TPU v7x, 32 devices: a whole 2x2x4 slice. The times are simulated.
32 devices in a mesh: row: 4 (over x, core), col: 2 (over y), chan: 4 (over z).
Axes of the slice: x: 2, y: 2, z: 4, core: 2. Of those that a mesh axis runs over, the one named last changes fastest.
Arguments:
- features: bfloat16 [2048, 72, 36], P('chan', 'row', 'col'), may hold values from -6 to 6
- dilated_weight: bfloat16 [3, 3, 3, 2048, 256], P(None, None, None, 'chan'), may hold values from -0.0625 to 0.0625
- point_weight: bfloat16 [2048, 256], P('chan'), may hold values from -0.1875 to 0.1875
- branch_gain: float32 [256, 4], P('chan'), may hold values from 0.5 to 2
- branch_shift: float32 [256, 4], P('chan'), may hold values from -3 to 3
- project_weight: bfloat16 [256, 4, 256], P('chan'), may hold values from -0.25 to 0.25
- project_shift: float32 [256], P('chan'), may hold values from -3 to 3
- cotangent: bfloat16 [256, 72, 36], P('chan', 'row', 'col'), may hold values from -6 to 6
Outputs:
- mixed_out: bfloat16 [256, 72, 36], P('chan', 'row', 'col')
- input_grad: bfloat16 [2048, 72, 36], P('chan', 'row', 'col')
- dilated_grad: bfloat16 [3, 3, 3, 2048, 256], P(None, None, None, 'chan')
- point_grad: bfloat16 [2048, 256], P('chan')
- project_grad: bfloat16 [256, 4, 256], P('chan')
All inputs are finite; a program needn't handle non-finite values.
Results may differ from a plain program's by a relative error of at most 0.007.
Values may be sent and summed in bfloat16 or wider, within the bound.
A program may use at most 128 MiB of HBM per device.

v0:
```python
import jax
import jax.numpy as jnp
from jax import lax
from jax.sharding import PartitionSpec as P

RATE_STEP = 6


def padded_2(cells, sides, width):
    for axis, dim in sides:
        count = lax.axis_size(axis)
        ends = count - 1
        head = lax.slice_in_dim(cells, 0, width, axis=dim)
        tail = lax.slice_in_dim(cells, cells.shape[dim] - width, cells.shape[dim], axis=dim)
        cells = jnp.concatenate(
            [
                lax.ppermute(tail, axis, [(i, (i + 1) % count) for i in range(ends)]),
                cells,
                lax.ppermute(head, axis, [((i + 1) % count, i) for i in range(ends)]),
            ],
            axis=dim,
        )
    return cells


def silu_slope(values):
    logistic = jax.nn.sigmoid(values)
    return logistic * (1.0 + values * (1.0 - logistic))


def tap_window(padded, top, left, tile_h, tile_w):
    return padded[:, top : top + tile_h, left : left + tile_w].reshape(
        padded.shape[0], tile_h * tile_w
    )


def per_device(
    features,
    dilated_weight,
    point_weight,
    branch_gain,
    branch_shift,
    project_weight,
    project_shift,
    cotangent,
):
    local_in, tile_h, tile_w = features.shape
    out_count = point_weight.shape[1]
    local_out = branch_gain.shape[0]
    pixels = tile_h * tile_w
    margin = 3 * RATE_STEP
    padded = padded_2(features, (("row", 1), ("col", 2)), margin)
    center = tap_window(padded, margin, margin, tile_h, tile_w)
    tap_views = []
    for branch in range(3):
        dilation = (branch + 1) * RATE_STEP
        for row_tap in range(3):
            for col_tap in range(3):
                tap_views.append(
                    tap_window(
                        padded,
                        margin + (row_tap - 1) * dilation,
                        margin + (col_tap - 1) * dilation,
                        tile_h,
                        tile_w,
                    )
                )
    stacked = jnp.stack(tap_views).reshape(3, 9 * local_in, pixels)
    weight_stack = dilated_weight.reshape(3, 9 * local_in, out_count)
    weight_slice = weight_stack
    dilated_part = jnp.einsum(
        "bko,bkp->obp", weight_slice, stacked, preferred_element_type=jnp.float32
    )
    point_part = jnp.einsum("co,cp->op", point_weight, center, preferred_element_type=jnp.float32)
    branch_pre = lax.psum_scatter(
        jnp.concatenate([point_part[:, None, :], dilated_part], axis=1),
        "chan",
        scatter_dimension=0,
        tiled=True,
    )
    branch_act = branch_pre * branch_gain[:, :, None] + branch_shift[:, :, None]
    hidden = jax.nn.silu(branch_act).astype(jnp.bfloat16)
    weight_slice = project_weight
    mixed = lax.psum_scatter(
        jnp.einsum("obq,obp->qp", weight_slice, hidden, preferred_element_type=jnp.float32),
        "chan",
        scatter_dimension=0,
        tiled=True,
    )
    mixed_act = mixed + project_shift[:, None]
    mixed_out = jax.nn.silu(mixed_act).astype(jnp.bfloat16).reshape(local_out, tile_h, tile_w)
    mixed_grad = (
        cotangent.reshape(local_out, pixels).astype(jnp.float32) * silu_slope(mixed_act)
    ).astype(jnp.bfloat16)
    shard_rows = lax.all_gather(mixed_grad, "chan", axis=0, tiled=True)
    weight_slice = project_weight
    hidden_total = jnp.einsum(
        "obq,qp->obp", weight_slice, shard_rows, preferred_element_type=jnp.float32
    )
    weight_block = jnp.einsum("obp,qp->obq", hidden, shard_rows, preferred_element_type=jnp.float32)
    project_total = weight_block
    hidden_grad, project_total = (hidden_total, project_total)
    branch_grad = (hidden_grad * silu_slope(branch_act) * branch_gain[:, :, None]).astype(
        jnp.bfloat16
    )
    gathered = lax.all_gather(branch_grad, "chan", axis=0, tiled=True)
    point_total = jnp.einsum(
        "cp,op->co", center, gathered[:, 0], preferred_element_type=jnp.float32
    )
    dilated_total = jnp.einsum(
        "bkp,obp->bko", stacked, gathered[:, 1:], preferred_element_type=jnp.float32
    )
    grad_grid = gathered[:, 1:].reshape(out_count, 3, tile_h, tile_w)
    spread = padded_2(grad_grid, (("row", 2), ("col", 3)), margin)
    back_views = []
    for branch in range(3):
        dilation = (branch + 1) * RATE_STEP
        for row_tap in range(3):
            for col_tap in range(3):
                top = margin - (row_tap - 1) * dilation
                left = margin - (col_tap - 1) * dilation
                back_views.append(
                    spread[:, branch, top : top + tile_h, left : left + tile_w].reshape(
                        out_count, pixels
                    )
                )
    back_stack = jnp.stack(back_views).reshape(3, 9, out_count, pixels)
    grad_total = jnp.einsum(
        "bkco,bkop->cp",
        dilated_weight.reshape(3, 9, local_in, out_count),
        back_stack,
        preferred_element_type=jnp.float32,
    )
    grad_total = grad_total + jnp.einsum(
        "co,op->cp", point_weight, gathered[:, 0], preferred_element_type=jnp.float32
    )
    grad_input = grad_total.reshape(local_in, tile_h, tile_w)
    dilated_part, point_part, project_part = (
        lax.psum_scatter(dilated_total, ("row", "col"), scatter_dimension=2, tiled=True),
        lax.psum_scatter(point_total, ("row", "col"), scatter_dimension=1, tiled=True),
        lax.psum_scatter(project_total, ("row", "col"), scatter_dimension=2, tiled=True),
    )
    dilated_round, point_round, project_round = (
        lax.all_gather(dilated_part.astype(jnp.bfloat16), ("row", "col"), axis=2, tiled=True),
        lax.all_gather(point_part.astype(jnp.bfloat16), ("row", "col"), axis=1, tiled=True),
        lax.all_gather(project_part.astype(jnp.bfloat16), ("row", "col"), axis=2, tiled=True),
    )
    dilated_grad = dilated_round.reshape(3, 3, 3, local_in, out_count)
    return (mixed_out, grad_input.astype(jnp.bfloat16), dilated_grad, point_round, project_round)


def solution(mesh):
    placed = (
        P("chan", "row", "col"),
        P(None, None, None, "chan", None),
        P("chan", None),
        P("chan", None),
        P("chan", None),
        P("chan", None, None),
        P("chan"),
        P("chan", "row", "col"),
    )
    return jax.shard_map(
        per_device,
        mesh=mesh,
        in_specs=placed,
        out_specs=(
            P("chan", "row", "col"),
            P("chan", "row", "col"),
            P(None, None, None, "chan", None),
            P("chan", None),
            P("chan", None, None),
        ),
        check_vma=False,
    )
```

profile of v0, /device:TPU:0, one launch (start us, length us, event | category | flops | bytes accessed | tf_op | source)
XLA Modules:
  0.0 543.7 jit_solution(16730396367815597802)
XLA Ops:
  8.4 2.4 collective-permute-start
  12.1 4.4 collective-permute-done.1
  17.8 4.4 collective-permute-start.2
  26.8 1.8 pad_maximum_fusion.4
  29.5 1.8 stack_reshape.78
  31.3 1.9 copy.98
  33.2 1.8 stack_reshape.84
  35.1 1.9 copy.101
  37.0 1.9 stack_reshape.87
  38.8 1.9 copy.106
  40.7 1.9 stack_reshape.92
  43.4 1.9 stack_reshape.95
  46.1 1.8 stack_reshape.100
  48.0 2.5 pad_maximum_fusion
  50.4 3.0 fusion.15
  54.4 1.7 constant_dynamic-update-slice_fusion.26
  71.8 1.9 constant_dynamic-update-slice_fusion.25
  75.4 1.7 constant_dynamic-update-slice_fusion.23
  77.9 1.7 constant_dynamic-update-slice_fusion.21
  79.6 1.7 constant_dynamic-update-slice_fusion.20
  90.5 2.5 fusion.19
  97.1 1.8 constant_dynamic-update-slice_fusion.12
  98.9 1.7 constant_dynamic-update-slice_fusion.11
  100.6 1.7 constant_dynamic-update-slice_fusion.10
  102.4 1.7 constant_dynamic-update-slice_fusion.9
  104.1 1.7 constant_dynamic-update-slice_fusion.8
  106.6 1.7 constant_dynamic-update-slice_fusion.6
  113.6 13.2 %copy.116 = bf16[27,512,324]{2,1,0:T(8,128)(2,1)} copy(bf16[27,512,324]{1,2,0:T(8,128)(2,1)} %constant_dynamic-update-slice_fusion) | data formatting | bytes 17915904 | tf_op jit(solution)/shard_map/stack | solution.py:68
  126.8 9.7 %convolution_bitcast_fusion = f32[256,3,324]{0,2,1:T(8,128)S(1)} fusion(bf16[3,4608,324]{2,1,0:T(8,128)(2,1)} %bitcast.165, bf16[3,4608,256]{2,1,0:T(8,128)(2,1)} %bitcast.169), kind=kOutput, calls=%fused_computation.3 | convolution fusion | flops 2293235712 | bytes 17031168 | tf_op jit(solution)/shard_map/bko,bkp->obp/dot_general | solution.py:71
  139.5 75.1 %all-reduce.3.cloned.1.call-done = f32[256,4,324]{2,1,0:T(4,128)} async-done(((f32[256,4,324]{2,1,0:T(4,128)}), f32[256,4,324]{2,1,0:T(4,128)}) %all-reduce.3.cloned.1.call-update) | async-done | bytes 1327120
  217.1 20.0 %reduce-scatter.13.cloned.1.call-done = f32[64,324]{1,0:T(8,128)} async-done(((f32[256,324]{1,0:T(8,128)}), f32[64,324]{1,0:T(8,128)}) %reduce-scatter.13.cloned.1.call-update) | async-done | bytes 82960
  238.4 13.7 %all_gather.15 = bf16[256,324]{1,0:T(8,128)(2,1)S(1)} all-gather(bf16[64,324]{1,0:T(8,128)(2,1)S(1)} %copy.121), channel_id=1, replica_groups=mesh['row'=4,'col'=2,'chan'=4] {'chan'}, dimensions={0}, use_global_device_ids=true | all-gather | bytes 207360 | tf_op jit(solution)/shard_map/all_gather | solution.py:95
  252.7 16.7 %all_gather.16 = bf16[256,4,324]{2,1,0:T(4,128)(2,1)S(1)} all-gather(bf16[64,4,324]{2,1,0:T(4,128)(2,1)S(1)} %copy.123), channel_id=1, replica_groups=mesh['row'=4,'col'=2,'chan'=4] {'chan'}, dimensions={0}, use_global_device_ids=true | all-gather | bytes 829440 | tf_op jit(solution)/shard_map/all_gather | solution.py:106
  270.5 13.7 %fusion.21 = f32[3,4608,256]{1,2,0:T(8,128)} fusion(bf16[3,4608,324]{2,1,0:T(8,128)(2,1)} %bitcast.166, bf16[256,3,324]{0,2,1:T(8,128)(2,1)S(1)} %copy.164), kind=kOutput, calls=%fused_computation.120 | convolution fusion | flops 2293235712 | bytes 23611392 | tf_op jit(solution)/shard_map/bkp,obp->bko/dot_general | solution.py:110
  288.3 96.2 %reduce-scatter.7.cloned.1.call-done = f32[3,4608,32]{1,2,0:T(8,128)} async-done(((f32[3,4608,256]{1,2,0:T(8,128)}), f32[3,4608,32]{1,2,0:T(8,128)}) %reduce-scatter.7.cloned.1.call-update) | async-done | bytes 1769488 | tf_op jit(solution)/shard_map/reduce_scatter | solution.py:139
  384.6 2.5 convert_element_type.45
  387.3 1.8 collective-permute-start.4
  390.8 3.4 collective-permute-done.5
  394.2 1.8 pad_maximum_fusion.1
  396.1 3.8 collective-permute-start.7
  406.6 16.7 %reduce-scatter.11.cloned.1.call-done = f32[64,4,32]{0,2,1:T(8,128)} async-done(((f32[64,4,256]{0,2,1:T(8,128)}), f32[64,4,32]{0,2,1:T(8,128)}) %reduce-scatter.11.cloned.1.call-update) | async-done | bytes 32784 | tf_op jit(solution)/shard_map/reduce_scatter | solution.py:141
  424.2 26.7 %all_gather.19 = bf16[64,4,256]{0,2,1:T(8,128)(2,1)S(1)} all-gather(bf16[64,4,32]{0,2,1:T(8,128)(2,1)S(1)} %convert_element_type.47), channel_id=1, replica_groups=mesh['row'=4,'col'=2,'chan'=4] {'row','col'}, dimensions={2}, use_global_device_ids=true | all-gather | bytes 147456 | tf_op jit(solution)/shard_map/all_gather | solution.py:146
  461.4 17.2 %all_gather.18 = bf16[512,256]{0,1:T(8,128)(2,1)S(1)} all-gather(bf16[512,32]{0,1:T(8,128)(2,1)S(1)} %convert_element_type.46), channel_id=1, replica_groups=mesh['row'=4,'col'=2,'chan'=4] {'row','col'}, dimensions={1}, use_global_device_ids=true | all-gather | bytes 294912 | tf_op jit(solution)/shard_map/all_gather | solution.py:145
  479.4 2.8 fusion.17
  483.0 2.5 pad_maximum_fusion.10
  486.3 2.7 pad_maximum_fusion.21
  519.8 5.6 %convolution_bitcast_fusion.1 = f32[324,512]{1,0:T(8,128)S(1)} fusion(bf16[3,9,256,324]{2,3,1,0:T(8,128)(2,1)S(1)} %bitcast.168, bf16[3,9,512,256]{3,2,1,0:T(8,128)(2,1)} %bitcast.170), kind=kOutput, calls=%fused_computation.5 | convolution fusion | flops 2293235712 | bytes 12220416 | tf_op jit(solution)/shard_map/bkco,bkop->cp/dot_general | solution.py:128
  526.6 10.3 %copy.156 = bf16[3,4608,256]{2,1,0:T(8,128)(2,1)} copy(bf16[3,4608,256]{1,2,0:T(8,128)(2,1)} %all-gather.2.cloned.1.call-done) | data formatting | bytes 14155776 | tf_op jit(solution)/shard_map/all_gather | solution.py:144
  (264 shorter events, 115.0 us)
Async XLA Ops:
  7.2 18.6 %copy-start = (bf16[512,256]{1,0:T(8,128)(2,1)S(1)}, bf16[512,256]{1,0:T(8,128)(2,1)}, u32[]{:S(2)}) copy-start(bf16[512,256]{1,0:T(8,128)(2,1)} %param.10) | copy-start | bytes 786436
  7.2 207.4 %all-reduce.3.cloned.1.call-start = ((), (), s32[]{:S(2)}) async-start(), calls=%async_computation.9 | async-start | bytes 3145728
  8.4 3.8 collective-permute-start
  10.8 5.8 %collective-permute-start.1 = (bf16[512,18,18]{0,1,2:T(8,128)(2,1)S(1)}, bf16[512,18,18]{0,1,2:T(8,128)(2,1)S(1)}, u32[]{:S(2)}, u32[]{:S(2)}) collective-permute-start(bf16[512,18,18]{0,1,2:T(8,128)(2,1)S(1)} %copy.87), channel_id=1, source_target_pairs={{8,0},{16,8},{24,16},{9,1},{17,9},{25,17},{10,2},{18,10},{26,18},{... | collective-permute-start | bytes 995336 | tf_op jit(solution)/shard_map/ppermute | solution.py:19
  17.8 30.1 %collective-permute-start.2 = (bf16[512,54,18]{0,1,2:T(8,128)(2,1)}, bf16[512,54,18]{0,1,2:T(8,128)(2,1)}, u32[]{:S(2)}, u32[]{:S(2)}) collective-permute-start(bf16[512,54,18]{0,1,2:T(8,128)(2,1)} %pad_maximum_fusion.3), channel_id=1, source_target_pairs={{0,4},{1,5},{2,6},{3,7},{8,12},{9,13},{10,14},{11,15},{16,20},{17,... | collective-permute-start | bytes 2985992 | tf_op jit(solution)/shard_map/ppermute | solution.py:17
  22.3 25.7 %collective-permute-start.3 = (bf16[512,54,18]{0,1,2:T(8,128)(2,1)}, bf16[512,54,18]{0,1,2:T(8,128)(2,1)S(1)}, u32[]{:S(2)}, u32[]{:S(2)}) collective-permute-start(bf16[512,54,18]{0,1,2:T(8,128)(2,1)} %pad_maximum_fusion.3), channel_id=1, source_target_pairs={{4,0},{5,1},{6,2},{7,3},{12,8},{13,9},{14,10},{15,11},{20,16},{21,... | collective-permute-start | bytes 2985992 | tf_op jit(solution)/shard_map/ppermute | solution.py:19
  71.8 11.3 %copy-start.6 = (bf16[1,512,324]{1,2,0:T(8,128)(2,1)S(1)}, bf16[1,512,324]{1,2,0:T(8,128)(2,1)}, u32[]{:S(2)}) copy-start(bf16[1,512,324]{1,2,0:T(8,128)(2,1)} %stack_reshape.85) | copy-start | bytes 995332
  71.8 12.1 %copy-start.8 = (bf16[1,512,324]{1,2,0:T(8,128)(2,1)S(1)}, bf16[1,512,324]{1,2,0:T(8,128)(2,1)}, u32[]{:S(2)}) copy-start(bf16[1,512,324]{1,2,0:T(8,128)(2,1)} %stack_reshape.86) | copy-start | bytes 995332
  71.8 12.8 %copy-start.4 = (bf16[1,512,324]{1,2,0:T(8,128)(2,1)S(1)}, bf16[1,512,324]{1,2,0:T(8,128)(2,1)}, u32[]{:S(2)}) copy-start(bf16[1,512,324]{1,2,0:T(8,128)(2,1)} %stack_reshape.87) | copy-start | bytes 995332
  71.8 13.6 %copy-start.5 = (bf16[1,512,324]{1,2,0:T(8,128)(2,1)S(1)}, bf16[1,512,324]{1,2,0:T(8,128)(2,1)}, u32[]{:S(2)}) copy-start(bf16[1,512,324]{1,2,0:T(8,128)(2,1)} %stack_reshape.88) | copy-start | bytes 995332
  71.8 14.3 %copy-start.7 = (bf16[1,512,324]{1,2,0:T(8,128)(2,1)S(1)}, bf16[1,512,324]{1,2,0:T(8,128)(2,1)}, u32[]{:S(2)}) copy-start(bf16[1,512,324]{1,2,0:T(8,128)(2,1)} %stack_reshape.89) | copy-start | bytes 995332
  71.8 15.9 %copy-start.1 = (bf16[512,18,18]{0,1,2:T(8,128)(2,1)S(1)}, bf16[512,18,18]{0,1,2:T(8,128)(2,1)}, u32[]{:S(2)}) copy-start(bf16[512,18,18]{0,1,2:T(8,128)(2,1)} %get-tuple-element.38) | copy-start | bytes 995332
  94.2 11.6 %copy-start.3 = (bf16[1,512,324]{1,2,0:T(8,128)(2,1)S(1)}, bf16[1,512,324]{1,2,0:T(8,128)(2,1)}, u32[]{:S(2)}) copy-start(bf16[1,512,324]{1,2,0:T(8,128)(2,1)} %stack_reshape.95) | copy-start | bytes 995332
  97.1 11.2 %copy-start.9 = (bf16[1,512,324]{1,2,0:T(8,128)(2,1)S(1)}, bf16[1,512,324]{1,2,0:T(8,128)(2,1)}, u32[]{:S(2)}) copy-start(bf16[1,512,324]{1,2,0:T(8,128)(2,1)} %stack_reshape.97) | copy-start | bytes 995332
  105.8 6.2 %copy-start.2 = (bf16[1,512,324]{1,2,0:T(8,128)(2,1)S(1)}, bf16[1,512,324]{1,2,0:T(8,128)(2,1)}, u32[]{:S(2)}) copy-start(bf16[1,512,324]{1,2,0:T(8,128)(2,1)} %stack_reshape.100) | copy-start | bytes 995332
  126.8 9.7 %copy-start.10 = (f32[256,1,324]{0,2,1:T(8,128)S(1)}, f32[256,1,324]{0,2,1:T(8,128)}, u32[]{:S(2)}) copy-start(f32[256,1,324]{0,2,1:T(8,128)} %convolution_bitcast_fusion.4) | copy-start | bytes 995332
  136.5 1.8 copy-start.35
  136.5 79.2 %copy-start.32 = (bf16[64,4,256]{2,1,0:T(4,128)(2,1)S(1)}, bf16[64,4,256]{2,1,0:T(4,128)(2,1)}, u32[]{:S(2)}) copy-start(bf16[64,4,256]{2,1,0:T(4,128)(2,1)} %param.13) | copy-start | bytes 393220
  136.5 79.2 %copy-start.33 = (f32[64,4]{0,1:T(4,128)S(1)}, f32[64,4]{0,1:T(4,128)}, u32[]{:S(2)}) copy-start(f32[64,4]{0,1:T(4,128)} %param.12) | copy-start | bytes 3076
  136.5 79.2 %copy-start.34 = (f32[64,4]{0,1:T(4,128)S(1)}, f32[64,4]{0,1:T(4,128)}, u32[]{:S(2)}) copy-start(f32[64,4]{0,1:T(4,128)} %param.11) | copy-start | bytes 3076
  136.6 80.4 %copy-start.30 = (bf16[64,18,18]{0,2,1:T(8,128)(2,1)S(1)}, bf16[64,18,18]{0,2,1:T(8,128)(2,1)}, u32[]{:S(2)}) copy-start(bf16[64,18,18]{0,2,1:T(8,128)(2,1)} %param.15) | copy-start | bytes 124420
  136.7 101.5 %copy-start.31 = (f32[64]{0:T(128)S(1)}, f32[64]{0:T(128)}, u32[]{:S(2)}) copy-start(f32[64]{0:T(128)} %param.14) | copy-start | bytes 772
  138.2 98.9 %reduce-scatter.13.cloned.1.call-start = ((), (), s32[]{:S(2)}) async-start(), calls=%async_computation.8 | async-start | bytes 491520
  217.0 167.5 %reduce-scatter.7.cloned.1.call-start = ((), (), s32[]{:S(2)}) async-start(), calls=%async_computation.4 | async-start | bytes 15925248 | tf_op jit(solution)/shard_map/reduce_scatter | solution.py:139
  284.2 139.2 %reduce-scatter.11.cloned.1.call-start = ((), (), s32[]{:S(2)}) async-start(), calls=%async_computation.7 | async-start | bytes 589824 | tf_op jit(solution)/shard_map/reduce_scatter | solution.py:141
  286.4 174.2 %reduce-scatter.9.cloned.1.call-start = ((), (), s32[]{:S(2)}) async-start(), calls=%async_computation.6 | async-start | bytes 589824 | tf_op jit(solution)/shard_map/reduce_scatter | solution.py:140
  288.3 238.3 %all-gather.2.cloned.1.call-start = ((), (), s32[]{:S(2)}) async-start(), calls=%async_computation.5 | async-start | bytes 7962624 | tf_op jit(solution)/shard_map/all_gather | solution.py:144
  387.3 3.5 collective-permute-start.4
  389.1 5.1 collective-permute-start.5
  396.1 83.4 %collective-permute-start.7 = (bf16[256,3,54,18]{0,2,3,1:T(8,128)(2,1)}, bf16[256,3,54,18]{0,2,3,1:T(8,128)(2,1)}, u32[]{:S(2)}, u32[]{:S(2)}) collective-permute-start(bf16[256,3,54,18]{0,2,3,1:T(8,128)(2,1)} %pad_maximum_fusion.1), channel_id=1, source_target_pairs={{0,4},{1,5},{2,6},{3,7},{8,12},{9,13},{10,14},{11,15},{16,20},{17,... | collective-permute-start | bytes 4478984 | tf_op jit(solution)/shard_map/ppermute | solution.py:17
  399.8 83.1 %collective-permute-start.6 = (bf16[256,3,54,18]{0,2,3,1:T(8,128)(2,1)}, bf16[256,3,54,18]{0,2,3,1:T(8,128)(2,1)}, u32[]{:S(2)}, u32[]{:S(2)}) collective-permute-start(bf16[256,3,54,18]{0,2,3,1:T(8,128)(2,1)} %pad_maximum_fusion.1), channel_id=1, source_target_pairs={{4,0},{5,1},{6,2},{7,3},{12,8},{13,9},{14,10},{15,11},{20,16},{21,... | collective-permute-start | bytes 4478984 | tf_op jit(solution)/shard_map/ppermute | solution.py:19
  489.0 9.8 %copy-start.14 = (bf16[256,1,18,18]{0,2,3,1:T(8,128)(2,1)S(1)}, bf16[256,1,18,18]{0,2,3,1:T(8,128)(2,1)}, u32[]{:S(2)}) copy-start(bf16[256,1,18,18]{0,2,3,1:T(8,128)(2,1)} %get-tuple-element.58) | copy-start | bytes 497668
  489.0 10.6 %copy-start.18 = (bf16[256,1,18,18]{0,2,3,1:T(8,128)(2,1)S(1)}, bf16[256,1,18,18]{0,2,3,1:T(8,128)(2,1)}, u32[]{:S(2)}) copy-start(bf16[256,1,18,18]{0,2,3,1:T(8,128)(2,1)} %get-tuple-element.30) | copy-start | bytes 497668
  489.0 11.4 %copy-start.12 = (bf16[256,1,18,18]{0,2,3,1:T(8,128)(2,1)S(1)}, bf16[256,1,18,18]{0,2,3,1:T(8,128)(2,1)}, u32[]{:S(2)}) copy-start(bf16[256,1,18,18]{0,2,3,1:T(8,128)(2,1)} %get-tuple-element.59) | copy-start | bytes 497668
  489.0 12.1 %copy-start.16 = (bf16[256,1,18,18]{0,2,3,1:T(8,128)(2,1)S(1)}, bf16[256,1,18,18]{0,2,3,1:T(8,128)(2,1)}, u32[]{:S(2)}) copy-start(bf16[256,1,18,18]{0,2,3,1:T(8,128)(2,1)} %get-tuple-element.29) | copy-start | bytes 497668
  489.0 12.9 %copy-start.11 = (bf16[256,1,18,18]{0,2,3,1:T(8,128)(2,1)S(1)}, bf16[256,1,18,18]{0,2,3,1:T(8,128)(2,1)}, u32[]{:S(2)}) copy-start(bf16[256,1,18,18]{0,2,3,1:T(8,128)(2,1)} %get-tuple-element.60) | copy-start | bytes 497668
  489.0 13.6 %copy-start.17 = (bf16[256,1,18,18]{0,2,3,1:T(8,128)(2,1)S(1)}, bf16[256,1,18,18]{0,2,3,1:T(8,128)(2,1)}, u32[]{:S(2)}) copy-start(bf16[256,1,18,18]{0,2,3,1:T(8,128)(2,1)} %get-tuple-element.53) | copy-start | bytes 497668
  491.9 11.7 %copy-start.15 = (bf16[256,1,18,18]{0,2,3,1:T(8,128)(2,1)S(1)}, bf16[256,1,18,18]{0,2,3,1:T(8,128)(2,1)}, u32[]{:S(2)}) copy-start(bf16[256,1,18,18]{0,2,3,1:T(8,128)(2,1)} %get-tuple-element.52) | copy-start | bytes 497668
  495.3 9.2 %copy-start.13 = (bf16[256,1,18,18]{0,2,3,1:T(8,128)(2,1)S(1)}, bf16[256,1,18,18]{0,2,3,1:T(8,128)(2,1)}, u32[]{:S(2)}) copy-start(bf16[256,1,18,18]{0,2,3,1:T(8,128)(2,1)} %get-tuple-element.51) | copy-start | bytes 497668
  499.6 9.5 %copy-start.23 = (bf16[1,256,324]{1,2,0:T(8,128)(2,1)S(1)}, bf16[1,256,324]{1,2,0:T(8,128)(2,1)}, u32[]{:S(2)}) copy-start(bf16[1,256,324]{1,2,0:T(8,128)(2,1)} %stack_reshape_squeeze.85) | copy-start | bytes 497668
  501.1 9.9 %copy-start.25 = (bf16[1,256,324]{1,2,0:T(8,128)(2,1)S(1)}, bf16[1,256,324]{1,2,0:T(8,128)(2,1)}, u32[]{:S(2)}) copy-start(bf16[1,256,324]{1,2,0:T(8,128)(2,1)} %stack_reshape_squeeze.88) | copy-start | bytes 497668
  501.2 9.9 %copy-start.26 = (bf16[1,256,324]{1,2,0:T(8,128)(2,1)S(1)}, bf16[1,256,324]{1,2,0:T(8,128)(2,1)}, u32[]{:S(2)}) copy-start(bf16[1,256,324]{1,2,0:T(8,128)(2,1)} %stack_reshape_squeeze.89) | copy-start | bytes 497668
  502.7 12.2 %copy-start.20 = (bf16[1,256,324]{1,2,0:T(8,128)(2,1)S(1)}, bf16[1,256,324]{1,2,0:T(8,128)(2,1)}, u32[]{:S(2)}) copy-start(bf16[1,256,324]{1,2,0:T(8,128)(2,1)} %stack_reshape_squeeze.94) | copy-start | bytes 497668
  503.5 13.3 %copy-start.24 = (bf16[1,256,324]{1,2,0:T(8,128)(2,1)S(1)}, bf16[1,256,324]{1,2,0:T(8,128)(2,1)}, u32[]{:S(2)}) copy-start(bf16[1,256,324]{1,2,0:T(8,128)(2,1)} %stack_reshape_squeeze.97) | copy-start | bytes 497668
  504.4 14.3 %copy-start.22 = (bf16[1,256,324]{1,2,0:T(8,128)(2,1)S(1)}, bf16[1,256,324]{1,2,0:T(8,128)(2,1)}, u32[]{:S(2)}) copy-start(bf16[1,256,324]{1,2,0:T(8,128)(2,1)} %stack_reshape_squeeze.100) | copy-start | bytes 497668
  504.5 15.2 %copy-start.19 = (bf16[1,256,324]{1,2,0:T(8,128)(2,1)S(1)}, bf16[1,256,324]{1,2,0:T(8,128)(2,1)}, u32[]{:S(2)}) copy-start(bf16[1,256,324]{1,2,0:T(8,128)(2,1)} %stack_reshape_squeeze.103) | copy-start | bytes 497668
  505.3 14.5 %copy-start.21 = (bf16[1,256,324]{1,2,0:T(8,128)(2,1)S(1)}, bf16[1,256,324]{1,2,0:T(8,128)(2,1)}, u32[]{:S(2)}) copy-start(bf16[1,256,324]{1,2,0:T(8,128)(2,1)} %stack_reshape_squeeze.106) | copy-start | bytes 497668
  505.3 14.4 %copy-start.27 = (bf16[1,256,324]{1,2,0:T(8,128)(2,1)S(1)}, bf16[1,256,324]{1,2,0:T(8,128)(2,1)}, u32[]{:S(2)}) copy-start(bf16[1,256,324]{1,2,0:T(8,128)(2,1)} %stack_reshape_squeeze.105) | copy-start | bytes 497668
  (2 other events, 1.6 us)
Sparse Core Ops, SparseCore 0:
  138.4 76.2 all-reduce.2
  217.5 19.6 reduce-scatter.12
  284.3 100.1 reduce-scatter.6
  387.8 35.5 reduce-scatter.10
  426.3 34.2 reduce-scatter.8
  462.5 49.9 all-gather.1
where the time goes:
time: 547 us; the launch traced here: 544 us
  waiting for transfers between devices  218 us (40%)
  local copies, waits for them, and re-layouts  165 us (30%)
  blocking collectives  74.2 us (14%)
  matrix products  33.3 us (6%)
  other arithmetic  20.2 us (4%)
  starting transfers between devices  17.7 us (3%)
  between operations  15.7 us (3%)
    reduce_scatter x1, waiting for transfers between devices, per_device(): lax.psum_scatter(dilated_total, ('row', 'col'), scatter_dimension=2, tile...  96.2 us
    unnamed x8, waiting for transfers between devices  95.2 us
    unnamed x133, local copies, waits for them, and re-layouts  55.4 us
    another operation x27, local copies, waits for them, and re-layouts, per_device(): stacked = jnp.stack(tap_views).reshape(3, 9 * local_in, pixels)  39 us
    all_gather x1, blocking collectives, per_device(): lax.all_gather(project_part.astype(jnp.bfloat16), ('row', 'col'), axis=2,...  26.7 us
    slice x25, local copies, waits for them, and re-layouts, tap_window(): padded[:, top:top + tile_h, left:left + tile_w]  23.3 us
    another operation x28, local copies, waits for them, and re-layouts, per_device(): back_stack = jnp.stack(back_views).reshape(3, 9, out_count, pixels)  21.3 us
    all_gather x1, blocking collectives, per_device(): lax.all_gather(point_part.astype(jnp.bfloat16), ('row', 'col'), axis=1, t...  17.2 us
  transfers between devices with their start and end apart: 14, of which 9 were waited for; matrix products, arithmetic and copies ran while one was open for 18% of the time, Pallas kernels for 0%

commit v1 on v0

v1 whole, which is shorter than its diff:
```python
import functools

import jax
import jax.numpy as jnp
from jax import lax
from jax.experimental import pallas as pl
from jax.experimental.pallas import tpu as pltpu
from jax.sharding import PartitionSpec as P

RATE_STEP = 6
SLOT = 8
MARGIN_RUNS = 3
MARGIN_ROWS = 3 * RATE_STEP * SLOT
MESH = pl.DeviceIdType.MESH
VMEM = pltpu.VMEM
LIMIT = 67_000_000


def sigmoid(v):
    return 1.0 / (1.0 + jnp.exp(-v))


def silu_slope(values):
    logistic = jax.nn.sigmoid(values)
    return logistic * (1.0 + values * (1.0 - logistic))


def to_runs(cells):
    count, tile_h, tile_w = cells.shape
    runs = tile_w // RATE_STEP
    cells = cells.reshape(count, tile_h, runs, RATE_STEP)
    cells = jnp.pad(cells, ((0, 0), (0, 0), (0, 0), (0, SLOT - RATE_STEP)))
    return cells.transpose(2, 1, 3, 0).reshape(runs, tile_h * SLOT, count)


def from_runs(cells, tile_h, tile_w):
    runs = tile_w // RATE_STEP
    count = cells.shape[-1]
    cells = cells.reshape(runs, tile_h, SLOT, count)[:, :, :RATE_STEP]
    return cells.transpose(3, 1, 0, 2).reshape(count, tile_h, tile_w)


def spread_kernel(n_row, n_col, x_ref, out_ref, local_sem, send_sems, recv_sems):
    n_hi = n_row // 2
    row = lax.axis_index("row")
    col = lax.axis_index("col")
    hi, core = row // 2, row % 2
    runs, rows, _ = x_ref.shape
    first = (rows // 2 + 15) // 16 * 16
    starts, sizes = (0, first), (first, rows - first)

    hi_peer = [lax.rem(hi + d, n_hi) for d in range(n_hi)]
    hi_from = [lax.rem(hi - d + n_hi, n_hi) for d in range(n_hi)]
    col_peer = [lax.rem(col + d, n_col) for d in range(n_col)]
    col_from = [lax.rem(col - d + n_col, n_col) for d in range(n_col)]
    sibling = {"row": hi * 2 + 1 - core}
    partners = [sibling]
    partners += [{"row": hi_peer[d] * 2 + core} for d in range(1, n_hi)]
    partners += [{"col": col_peer[d]} for d in range(1, n_col)]

    barrier = pltpu.get_barrier_semaphore()
    for who in partners:
        pl.semaphore_signal(barrier, inc=1, device_id=who, device_id_type=MESH)

    dtype = out_ref.dtype
    total_runs, total_rows, width = out_ref.shape
    edge = jnp.zeros((MARGIN_ROWS, width), dtype)

    def clear_run(u, _):
        for at in (u, total_runs - MARGIN_RUNS + u):
            for y in range(0, total_rows, MARGIN_ROWS):
                out_ref[at, pl.ds(y, MARGIN_ROWS), :] = edge
        return 0

    def clear_ends(u, _):
        out_ref[u, pl.ds(0, MARGIN_ROWS), :] = edge
        out_ref[u, pl.ds(total_rows - MARGIN_ROWS, MARGIN_ROWS), :] = edge
        return 0

    pl.semaphore_wait(barrier, len(partners))

    def place(h, hi_, core_, col_):
        return out_ref.at[
            pl.ds(MARGIN_RUNS + runs * col_, runs),
            pl.ds(pl.multiple_of(MARGIN_ROWS + (hi_ * 2 + core_) * rows + starts[h], 16), sizes[h]),
            :,
        ]

    sent = []

    def send(h, dh, dc, who, slot):
        if dh == 0 and dc == 0:
            src = x_ref.at[:, pl.ds(starts[h], sizes[h]), :]
        else:
            src = place(h, hi_from[dh], core, col_from[dc])
        copy = pltpu.make_async_remote_copy(
            src_ref=src,
            dst_ref=place(h, hi_from[dh], core, col_from[dc]),
            send_sem=send_sems.at[len(sent)],
            recv_sem=recv_sems.at[slot],
            device_id=who,
            device_id_type=MESH,
        )
        copy.start()
        sent.append(copy)

    def slot_of(h, dh, dc, side):
        return ((h * n_hi + dh) * n_col + dc) * 2 + side

    def arrive(h, dh, dc, side):
        core_ = core if side == 0 else 1 - core
        here = place(h, hi_from[dh], core_, col_from[dc])
        pltpu.make_async_remote_copy(
            src_ref=here,
            dst_ref=here,
            send_sem=send_sems.at[0],
            recv_sem=recv_sems.at[slot_of(h, dh, dc, side)],
            device_id=sibling,
            device_id_type=MESH,
        ).wait_recv()

    for d in range(1, n_hi):
        send(0, 0, 0, {"row": hi_peer[d] * 2 + core}, slot_of(0, d, 0, 0))
    for d in range(1, n_col):
        send(1, 0, 0, {"col": col_peer[d]}, slot_of(1, 0, d, 0))
    for d in range(1, n_col):
        send(0, 0, 0, {"col": col_peer[d]}, slot_of(0, 0, d, 0))
    for d in range(1, n_hi):
        send(1, 0, 0, {"row": hi_peer[d] * 2 + core}, slot_of(1, d, 0, 0))
    for h in range(2):
        send(h, 0, 0, sibling, slot_of(h, 0, 0, 1))
    own = pltpu.make_async_copy(
        x_ref,
        out_ref.at[
            pl.ds(MARGIN_RUNS + runs * col, runs),
            pl.ds(pl.multiple_of(MARGIN_ROWS + row * rows, 16), rows),
            :,
        ],
        local_sem,
    )
    own.start()
    lax.fori_loop(0, MARGIN_RUNS, clear_run, 0)
    lax.fori_loop(MARGIN_RUNS, total_runs - MARGIN_RUNS, clear_ends, 0)

    for dh in range(1, n_hi):
        arrive(0, dh, 0, 0)
        for d in range(1, n_col):
            send(0, dh, 0, {"col": col_peer[d]}, slot_of(0, dh, d, 0))
        send(0, dh, 0, sibling, slot_of(0, dh, 0, 1))
    for dc in range(1, n_col):
        arrive(1, 0, dc, 0)
        for d in range(1, n_hi):
            send(1, 0, dc, {"row": hi_peer[d] * 2 + core}, slot_of(1, d, dc, 0))
        send(1, 0, dc, sibling, slot_of(1, 0, dc, 1))
    for dc in range(1, n_col):
        arrive(0, 0, dc, 0)
        send(0, 0, dc, sibling, slot_of(0, 0, dc, 1))
    for dh in range(1, n_hi):
        arrive(1, dh, 0, 0)
        send(1, dh, 0, sibling, slot_of(1, dh, 0, 1))
    for h in range(2):
        for dh in range(1, n_hi):
            for dc in range(1, n_col):
                arrive(h, dh, dc, 0)
                send(h, dh, dc, sibling, slot_of(h, dh, dc, 1))
    for h in range(2):
        for dh in range(n_hi):
            for dc in range(n_col):
                arrive(h, dh, dc, 1)
    own.wait()
    for copy in sent:
        copy.wait_send()


def spread(cells, collective_id):
    n_row, n_col = lax.axis_size("row"), lax.axis_size("col")
    runs, rows, width = cells.shape
    tiles = n_row // 2 * n_col
    shape = (runs * n_col + 2 * MARGIN_RUNS, rows * n_row + 2 * MARGIN_ROWS, width)
    copies = 2 * ((n_row // 2 - 1) + (n_col - 1) * (n_row // 2) + tiles) + 2 * tiles
    return pl.pallas_call(
        functools.partial(spread_kernel, n_row, n_col),
        out_shape=jax.ShapeDtypeStruct(shape, cells.dtype),
        in_specs=[pl.BlockSpec(memory_space=VMEM)],
        out_specs=pl.BlockSpec(memory_space=VMEM),
        scratch_shapes=[
            pltpu.SemaphoreType.DMA,
            pltpu.SemaphoreType.DMA((copies,)),
            pltpu.SemaphoreType.DMA((4 * tiles,)),
        ],
        compiler_params=pltpu.CompilerParams(
            collective_id=collective_id, has_side_effects=True, vmem_limit_bytes=LIMIT
        ),
        name="spread_tiles",
    )(cells)


def tap_of(t):
    tap = jnp.maximum(t - 1, 0)
    branch = jnp.where(t == 0, 0, tap // 9 + 1)
    inner = tap % 9
    down = jnp.where(t == 0, 0, (inner // 3 - 1) * branch)
    across = jnp.where(t == 0, 0, (inner % 3 - 1) * branch)
    return branch, down, across


def forward_kernel(runs, rows, x_ref, wp_ref, w_ref, out_ref, total):
    t = pl.program_id(0)
    branch, down, across = tap_of(t)
    u0 = MARGIN_RUNS + runs * lax.axis_index("col") + across
    y0 = MARGIN_ROWS + rows * lax.axis_index("row") + down * (RATE_STEP * SLOT)
    width = x_ref.shape[-1]
    window = x_ref[pl.ds(u0, runs), pl.ds(pl.multiple_of(y0, 16), rows), :].reshape(
        runs * rows, width
    )
    weight = jnp.where(t == 0, wp_ref[...], w_ref[0])
    part = jnp.dot(window, weight, preferred_element_type=jnp.float32)
    fresh = jnp.logical_or(t == 0, lax.rem(t - 1, 9) == 0)

    @pl.when(fresh)
    def _():
        total[...] = part

    @pl.when(jnp.logical_not(fresh))
    def _():
        total[...] += part

    @pl.when(lax.rem(t, 9) == 0)
    def _():
        used = runs * rows
        out_ref[0, pl.ds(0, used), :] = total[...].astype(out_ref.dtype)
        if out_ref.shape[1] > used:
            out_ref[0, pl.ds(used, out_ref.shape[1] - used), :] = jnp.zeros(
                (out_ref.shape[1] - used, out_ref.shape[2]), out_ref.dtype
            )


def forward(spread_x, point_weight, taps, runs, rows, padded):
    width, out_count = point_weight.shape
    return pl.pallas_call(
        functools.partial(forward_kernel, runs, rows),
        grid=(28,),
        out_shape=jax.ShapeDtypeStruct((4, padded, out_count), jnp.bfloat16),
        in_specs=[
            pl.BlockSpec(memory_space=VMEM),
            pl.BlockSpec(memory_space=VMEM),
            pl.BlockSpec((1, width, out_count), lambda t: (jnp.maximum(t - 1, 0), 0, 0)),
        ],
        out_specs=pl.BlockSpec((1, padded, out_count), lambda t: ((t + 8) // 9, 0, 0)),
        scratch_shapes=[VMEM((runs * rows, out_count), jnp.float32)],
        compiler_params=pltpu.CompilerParams(
            dimension_semantics=("arbitrary",), vmem_limit_bytes=LIMIT
        ),
        name="forward_taps",
    )(spread_x, point_weight, taps)


def middle_kernel(
    n_chan, part_ref, gain_ref, shift_ref, pw_ref, pshift_ref, cot_ref,
    out_ref, project_ref, grad_ref, landed, own, send_sems, recv_sems, send2, recv2, local_sem,
):
    me = lax.axis_index("chan")
    size = cot_ref.shape[0]
    width = gain_ref.shape[1]
    peers = [lax.rem(me + d, n_chan) for d in range(n_chan)]
    froms = [lax.rem(me - d + n_chan, n_chan) for d in range(n_chan)]
    barrier = pltpu.get_barrier_semaphore()
    for d in range(1, n_chan):
        pl.semaphore_signal(barrier, inc=1, device_id={"chan": peers[d]}, device_id_type=MESH)
    pl.semaphore_wait(barrier, n_chan - 1)
    copies = []
    for d in range(1, n_chan):
        copy = pltpu.make_async_remote_copy(
            src_ref=part_ref.at[:, pl.ds(pl.multiple_of(peers[d] * size, 16), size), :],
            dst_ref=landed.at[d - 1],
            send_sem=send_sems.at[d - 1],
            recv_sem=recv_sems.at[d - 1],
            device_id={"chan": peers[d]},
            device_id_type=MESH,
        )
        copy.start()
        copies.append(copy)
    for copy in copies:
        copy.wait_recv()
    acts = []
    mixed = jnp.zeros((size, width), jnp.float32)
    hiddens = []
    mine = pl.ds(pl.multiple_of(me * size, 16), size)
    for b in range(4):
        pre = part_ref[b, mine, :].astype(jnp.float32)
        for d in range(n_chan - 1):
            pre = pre + landed[d, b].astype(jnp.float32)
        act = pre * gain_ref[b][None, :] + shift_ref[b][None, :]
        hidden = (act * jax.nn.sigmoid(act)).astype(jnp.bfloat16)
        acts.append(act)
        hiddens.append(hidden)
        mixed = mixed + jnp.dot(hidden, pw_ref[b], preferred_element_type=jnp.float32)
    mixed_act = mixed + pshift_ref[...]
    logistic = jax.nn.sigmoid(mixed_act)
    out_ref[...] = (mixed_act * logistic).astype(jnp.bfloat16)
    mixed_grad = (
        cot_ref[...].astype(jnp.float32) * (logistic * (1.0 + mixed_act * (1.0 - logistic)))
    ).astype(jnp.bfloat16)
    for b in range(4):
        hidden_grad = lax.dot_general(
            mixed_grad, pw_ref[b], (((1,), (1,)), ((), ())), preferred_element_type=jnp.float32
        )
        own[:, b * width : (b + 1) * width] = (
            hidden_grad * silu_slope(acts[b]) * gain_ref[b][None, :]
        ).astype(jnp.bfloat16)
    place = grad_ref.at[mine, :]
    local = pltpu.make_async_copy(own, place, local_sem)
    local.start()
    grads = []
    for d in range(1, n_chan):
        copy = pltpu.make_async_remote_copy(
            src_ref=own,
            dst_ref=place,
            send_sem=send2.at[d - 1],
            recv_sem=recv2.at[d - 1],
            device_id={"chan": peers[d]},
            device_id_type=MESH,
        )
        copy.start()
        grads.append(copy)
    for b in range(4):
        project_ref[b] = lax.dot_general(
            hiddens[b], mixed_grad, (((0,), (0,)), ((), ())), preferred_element_type=jnp.float32
        )
    local.wait()
    for d in range(1, n_chan):
        there = grad_ref.at[pl.ds(pl.multiple_of(froms[d] * size, 16), size), :]
        pltpu.make_async_remote_copy(
            src_ref=own,
            dst_ref=there,
            send_sem=send2.at[d - 1],
            recv_sem=recv2.at[d - 1],
            device_id={"chan": peers[d]},
            device_id_type=MESH,
        ).wait_recv()
    for copy in copies + grads:
        copy.wait_send()


def middle(part, gain, shift, pw, pshift, cot):
    n_chan = lax.axis_size("chan")
    size, width = cot.shape
    vmem = pl.BlockSpec(memory_space=VMEM)
    dma = pltpu.SemaphoreType.DMA((n_chan - 1,))
    return pl.pallas_call(
        functools.partial(middle_kernel, n_chan),
        out_shape=(
            jax.ShapeDtypeStruct((size, width), jnp.bfloat16),
            jax.ShapeDtypeStruct((4, width, width), jnp.float32),
            jax.ShapeDtypeStruct((size * n_chan, 4 * width), jnp.bfloat16),
        ),
        in_specs=[vmem] * 6,
        out_specs=(vmem,) * 3,
        scratch_shapes=[
            VMEM((n_chan - 1, 4, size, width), jnp.bfloat16),
            VMEM((size, 4 * width), jnp.bfloat16),
            dma, dma, dma, dma,
            pltpu.SemaphoreType.DMA,
        ],
        compiler_params=pltpu.CompilerParams(
            collective_id=2, has_side_effects=True, vmem_limit_bytes=LIMIT
        ),
        name="middle",
    )(part, gain, shift, pw, pshift, cot)


def backward_kernel(runs, rows, xt_ref, b_ref, wp_ref, w_ref, point_ref, dil_ref, in_ref, total, grad):
    t = pl.program_id(0)
    branch, down, across = tap_of(t)
    pairs, width, depth = xt_ref.shape
    out_count = b_ref.shape[-1]
    full_rows = b_ref.shape[1] - 2 * MARGIN_ROWS
    y_off = pl.multiple_of(MARGIN_ROWS - down * (RATE_STEP * SLOT), 16)

    def step(g, _):
        cells = b_ref[pl.ds(MARGIN_RUNS - across + 2 * g, 2), pl.ds(y_off, full_rows), :]
        part = jnp.dot(
            xt_ref[g], cells.reshape(depth, out_count), preferred_element_type=jnp.float32
        )

        @pl.when(g == 0)
        def _():
            grad[...] = part

        @pl.when(g > 0)
        def _():
            grad[...] += part

        return 0

    lax.fori_loop(0, pairs, step, 0)

    @pl.when(t == 0)
    def _():
        point_ref[...] = grad[...].astype(jnp.bfloat16)

    @pl.when(t > 0)
    def _():
        dil_ref[0] = grad[...].astype(jnp.bfloat16)

    u0 = MARGIN_RUNS + runs * lax.axis_index("col") - across
    y0 = MARGIN_ROWS + rows * lax.axis_index("row") - down * (RATE_STEP * SLOT)
    window = b_ref[pl.ds(u0, runs), pl.ds(pl.multiple_of(y0, 16), rows), :].reshape(
        runs * rows, out_count
    )
    weight = jnp.where(t == 0, wp_ref[...], w_ref[0])
    part = lax.dot_general(
        window, weight, (((1,), (1,)), ((), ())), preferred_element_type=jnp.float32
    )

    @pl.when(t == 0)
    def _():
        total[...] = part

    @pl.when(t > 0)
    def _():
        total[...] += part

    @pl.when(t == 27)
    def _():
        in_ref[...] = total[...].astype(jnp.bfloat16)


def backward(xt, spread_b, point_weight, taps, runs, rows):
    width, out_count = point_weight.shape
    total_runs, total_rows, _ = spread_b.shape
    tap_index = lambda t: (jnp.maximum(t - 1, 0), 0, 0)
    return pl.pallas_call(
        functools.partial(backward_kernel, runs, rows),
        grid=(28,),
        out_shape=(
            jax.ShapeDtypeStruct((width, out_count), jnp.bfloat16),
            jax.ShapeDtypeStruct((27, width, out_count), jnp.bfloat16),
            jax.ShapeDtypeStruct((runs * rows, width), jnp.bfloat16),
        ),
        in_specs=[
            pl.BlockSpec(memory_space=VMEM),
            pl.BlockSpec((total_runs, total_rows, out_count), lambda t: (0, 0, (t + 8) // 9)),
            pl.BlockSpec(memory_space=VMEM),
            pl.BlockSpec((1, width, out_count), tap_index),
        ],
        out_specs=(
            pl.BlockSpec((width, out_count), lambda t: (0, 0)),
            pl.BlockSpec((1, width, out_count), tap_index),
            pl.BlockSpec((runs * rows, width), lambda t: (0, 0)),
        ),
        scratch_shapes=[
            VMEM((runs * rows, width), jnp.float32),
            VMEM((width, out_count), jnp.float32),
        ],
        compiler_params=pltpu.CompilerParams(
            dimension_semantics=("arbitrary",), vmem_limit_bytes=LIMIT
        ),
        name="backward_taps",
    )(xt, spread_b, point_weight, taps)


def per_device(
    features,
    dilated_weight,
    point_weight,
    branch_gain,
    branch_shift,
    project_weight,
    project_shift,
    cotangent,
):
    local_in, tile_h, tile_w = features.shape
    out_count = point_weight.shape[1]
    local_out = branch_gain.shape[0]
    n_chan = lax.axis_size("chan")
    me = lax.axis_index("chan")
    runs, rows = tile_w // RATE_STEP, tile_h * SLOT
    used = runs * rows
    size = (-(-used // n_chan) + 15) // 16 * 16
    padded = size * n_chan
    taps = dilated_weight.reshape(27, local_in, out_count)

    spread_x = spread(to_runs(features), 0)
    vectors = jnp.concatenate([branch_gain, branch_shift, project_shift[:, None]], axis=1)
    vectors = lax.all_gather(vectors, "chan", axis=0, tiled=True).T
    gain, shift, pshift = vectors[:4], vectors[4:8], vectors[8:9]
    pw = lax.all_gather(project_weight, "chan", axis=0, tiled=True).transpose(1, 0, 2)
    cot = to_runs(cotangent).reshape(used, local_out)
    cot = jnp.pad(cot, ((0, padded - used), (0, 0)))
    cot = lax.all_to_all(cot, "chan", split_axis=0, concat_axis=1, tiled=True)

    part = forward(spread_x, point_weight, taps, runs, rows, padded)
    mixed_out, project, grads = middle(part, gain, shift, pw, pshift, cot)
    spread_b = spread(grads[:used].reshape(runs, rows, 4 * out_count), 1)

    total_runs, total_rows, _ = spread_x.shape
    inner = spread_x[MARGIN_RUNS:-MARGIN_RUNS, MARGIN_ROWS:-MARGIN_ROWS]
    pairs = inner.shape[0] // 2
    xt = inner.reshape(pairs, 2 * inner.shape[1], local_in).transpose(0, 2, 1)
    point_grad, dilated_grad, input_grad = backward(
        xt, spread_b, point_weight, taps, runs, rows
    )

    mixed_out = lax.all_to_all(mixed_out, "chan", split_axis=1, concat_axis=0, tiled=True)
    mixed_out = from_runs(mixed_out[:used], tile_h, tile_w)
    project = lax.psum_scatter(project, "chan", scatter_dimension=1, tiled=True)
    project = lax.psum(project, ("row", "col")).astype(jnp.bfloat16).transpose(1, 0, 2)
    return (
        mixed_out,
        from_runs(input_grad, tile_h, tile_w),
        dilated_grad.reshape(dilated_weight.shape),
        point_grad,
        project,
    )


def solution(mesh):
    placed = (
        P("chan", "row", "col"),
        P(None, None, None, "chan", None),
        P("chan", None),
        P("chan", None),
        P("chan", None),
        P("chan", None, None),
        P("chan"),
        P("chan", "row", "col"),
    )
    return jax.shard_map(
        per_device,
        mesh=mesh,
        in_specs=placed,
        out_specs=(
            P("chan", "row", "col"),
            P("chan", "row", "col"),
            P(None, None, None, "chan", None),
            P("chan", None),
            P("chan", None, None),
        ),
        check_vma=False,
    )
```

time: 547 us -> 311 us (0.57)
  waiting for transfers between devices: 218 us -> 0.02 us
  Pallas kernels: 0 us -> 197 us
  local copies, waits for them, and re-layouts: 165 us -> 21.7 us
  matrix products: 33.3 us -> 0 us
  other arithmetic: 20.2 us -> 0.72 us
  blocking collectives: 74.2 us -> 59.8 us
    pallas_call x0 -> x5, Pallas kernels: none -> 197 us  [the longest x2 66.4 us: spread(): pl.pallas_call(functools.partial(spread_kernel, n_row, n_col), out_shape=...]
    reduce_scatter x3 -> x1, waiting for transfers between devices: 114 us -> 0.01 us  [per_device(): project = lax.psum_scatter(project, 'chan', scatter_dimension=1, tiled=True)]
    unnamed x8 -> x1, waiting for transfers between devices: 95.2 us -> 0.02 us
    another operation x55 -> x0, local copies, waits for them, and re-layouts: 60.2 us -> none  [the longest x27 39 us: per_device(): stacked = jnp.stack(tap_views).reshape(3, 9 * local_in, pixels)]
    unnamed x133 -> x4, local copies, waits for them, and re-layouts: 55.4 us -> 2.42 us
    all_gather x4 -> x2, blocking collectives: 74.2 us -> 30.3 us  [the longest x1 16.7 us: per_device(): lax.all_gather(project_weight, 'chan', axis=0, tiled=True)]
    dot_general x9 -> x0, matrix products: 33.3 us -> none  [the longest x1 13.7 us: per_device(): jnp.einsum('bkp,obp->bko', stacked, gathered[:, 1:], preferred_element_ty...]
    psum x0 -> x1, blocking collectives: none -> 29.5 us  [per_device(): lax.psum(project, ('row', 'col')).astype(jnp.bfloat16).transpose(1, 0, 2)]
  transfers between devices with their start and end apart: 14 -> 3, of which waited for: 9 -> 0; matrix products, arithmetic and copies ran while one was open for 18% -> 6% of each run, Pallas kernels for 0% -> 50%
where the time goes in v1:
time: 311 us; the launch traced here: 310 us
  Pallas kernels  197 us (63%)
  blocking collectives  59.8 us (19%)
  local copies, waits for them, and re-layouts  21.7 us (7%)
  starting transfers between devices  16 us (5%)
  between operations  14.1 us (5%)
    pallas_call x2, Pallas kernels, spread(): pl.pallas_call(functools.partial(spread_kernel, n_row, n_col), out_shape=...  66.4 us
    pallas_call x1, Pallas kernels, backward(): pl.pallas_call(functools.partial(backward_kernel, runs, rows), grid=(28,)...  65.9 us
    pallas_call x1, Pallas kernels, middle(): pl.pallas_call(functools.partial(middle_kernel, n_chan), out_shape=(jax.S...  41.7 us
    psum x1, blocking collectives, per_device(): lax.psum(project, ('row', 'col')).astype(jnp.bfloat16).transpose(1, 0, 2)  29.5 us
    pallas_call x1, Pallas kernels, forward(): pl.pallas_call(functools.partial(forward_kernel, runs, rows), grid=(28,),...  23.4 us
    all_gather x1, blocking collectives, per_device(): lax.all_gather(project_weight, 'chan', axis=0, tiled=True)  16.7 us
    all_gather x1, blocking collectives, per_device(): vectors = lax.all_gather(vectors, 'chan', axis=0, tiled=True).T  13.7 us
    all_to_all x1, starting transfers between devices, per_device(): lax.all_to_all(mixed_out, 'chan', split_axis=1, concat_axis=0, tiled=True)  9.69 us
  transfers between devices with their start and end apart: 3, of which 0 were waited for; matrix products, arithmetic and copies ran while one was open for 6% of the time, Pallas kernels for 50%

profile of v1, /device:TPU:0, one launch (start us, length us, event | category | flops | bytes accessed | tf_op | source)
XLA Modules:
  0.0 309.9 jit_solution(7093829112821916290)
XLA Ops:
  7.2 0.9 reshape.52
  8.2 0.7 copy.51
  8.9 6.3 %all-to-all-start = ((bf16[4,112,64]{1,2,0:T(8,128)(2,1)}), bf16[4,112,64]{1,2,0:T(8,128)(2,1)}, u32[]{:S(2)}, u32[]{:S(2)}) async-start(bf16[4,112,64]{1,2,0:T(8,128)(2,1)} %copy.51), calls=%async_computation | async-start | bytes 131072 | tf_op jit(solution)/shard_map/all_to_all | solution.py:491
  15.3 0.0 reduce-scatter.2.cloned.1.call-start
  15.3 0.7 maximum_bitcast_fusion
  16.0 13.7 %all-gather = f32[4,64,9]{1,2,0:T(8,128)S(1)} all-gather(f32[1,64,9]{1,2,0:T(8,128)S(1)} %maximum_bitcast_fusion), channel_id=1, replica_groups=mesh['row'=4,'col'=2,'chan'=4] {'chan'}, dimensions={0}, use_global_device_ids=true | all-gather | bytes 11520 | tf_op jit(solution)/shard_map/all_gather | solution.py:486
  29.7 0.1 reshape.61
  29.7 0.6 fusion
  30.3 0.9 copy.48
  31.3 1.1 reshape.49
  32.4 0.8 pad_bitcast_fusion.x_ref
  33.2 16.7 %all_gather.7 = bf16[256,4,256]{2,0,1:T(8,128)(2,1)} all-gather(bf16[64,4,256]{2,0,1:T(8,128)(2,1)S(1)} %copy.48), channel_id=1, replica_groups=mesh['row'=4,'col'=2,'chan'=4] {'chan'}, dimensions={0}, use_global_device_ids=true | all-gather | bytes 655360 | tf_op jit(solution)/shard_map/all_gather | solution.py:488
  49.9 0.5 slice.34.pshift_ref
  50.5 24.4 %spread_tiles.2.x_ref = bf16[12,864,512]{2,1,0:T(8,128)(2,1)} custom-call(bf16[3,144,512]{2,1,0:T(8,128)(2,1)} %pad_bitcast_fusion.x_ref), custom_call_target="tpu_custom_call" | custom-call | tf_op jit(solution)/shard_map/spread_tiles/pallas_call | solution.py:181
  74.9 23.4 %forward_taps.1.part_ref = bf16[4,448,256]{2,1,0:T(8,128)(2,1)} custom-call(bf16[12,864,512]{2,1,0:T(8,128)(2,1)} %spread_tiles.2.x_ref, bf16[512,256]{1,0:T(8,128)(2,1)} %wp_ref.3, bf16[27,512,256]{2,1,0:T(8,128)(2,1)} %bitcast.44), custom_call_target="tpu_custom_call" | custom-call | tf_op jit(solution)/shard_map/forward_taps/pallas_call | solution.py:240
  98.2 0.0 all-to-all-done
  98.2 1.6 copy.52.cot_ref
  99.8 41.7 %middle.1 = (bf16[112,256]{1,0:T(8,128)(2,1)}, f32[4,256,256]{2,1,0:T(8,128)}, bf16[448,1024]{1,0:T(8,128)(2,1)}) custom-call(bf16[4,448,256]{2,1,0:T(8,128)(2,1)} %forward_taps.1.part_ref, f32[4,256]{1,0:T(4,128)} %get-tuple-element.38.gain_ref, f32[4,256]{1,0:T(4,128)} %get-tuple-element.37.shift_ref, bf16[4,256,256]{2,1,0:T(8,128)(2,1)} %bitcast.49, ...), custom_call_target="tpu_custom_call" | custom-call | tf_op jit(solution)/shard_map/middle/pallas_call | solution.py:350
  141.5 0.0 reduce-scatter.2.cloned.1.call-update
  141.6 2.2 slice.29
  143.8 3.8 %copy.57 = bf16[3,1152,512]{1,2,0:T(8,128)(2,1)} copy(bf16[3,1152,512]{2,1,0:T(8,128)(2,1)S(1)} %bitcast.46) | data formatting | bytes 7077888 | tf_op jit(solution)/shard_map/reshape | solution.py:500
  147.6 1.6 copy.53
  149.2 9.7 %all-to-all-start.1 = ((bf16[112,4,64]{0,2,1:T(8,128)(2,1)}), bf16[112,4,64]{0,2,1:T(8,128)(2,1)}, u32[]{:S(2)}, u32[]{:S(2)}) async-start(bf16[112,4,64]{0,2,1:T(8,128)(2,1)} %bitcast.12), calls=%async_computation.1 | async-start | bytes 131072 | tf_op jit(solution)/shard_map/all_to_all | solution.py:505
  158.9 2.1 slice.30
  161.0 42.0 %spread_tiles.3.b_ref = bf16[12,864,1024]{2,1,0:T(8,128)(2,1)} custom-call(bf16[3,144,1024]{2,1,0:T(8,128)(2,1)} %bitcast.48), custom_call_target="tpu_custom_call" | custom-call | tf_op jit(solution)/shard_map/spread_tiles/pallas_call | solution.py:181
  203.0 65.9 %backward_taps.1 = (bf16[512,256]{1,0:T(8,128)(2,1)}, bf16[27,512,256]{2,1,0:T(8,128)(2,1)}, bf16[432,512]{1,0:T(8,128)(2,1)}) custom-call(bf16[3,512,1152]{2,1,0:T(8,128)(2,1)} %bitcast.47, bf16[12,864,1024]{2,1,0:T(8,128)(2,1)} %spread_tiles.3.b_ref, bf16[512,256]{1,0:T(8,128)(2,1)} %wp_ref.3, bf16[27,512,256]{2,1,0:T(8,128)(2,1)} %bitcast.45), custom_call_target="tpu_custom_call" | custom-call | tf_op jit(solution)/shard_map/backward_taps/pallas_call | solution.py:433
  269.0 1.0 slice_bitcast_fusion
  270.0 0.9 reshape.58
  270.9 0.0 all-to-all-done.1
  270.9 0.9 copy.54
  271.8 0.1 all_to_all.35
  271.9 0.1 copy.55
  272.1 0.7 copy.59
  272.8 0.0 reduce-scatter.2.cloned.1.call-done
  272.8 29.5 %all-reduce.4 = bf16[4,64,256]{2,1,0:T(8,128)(2,1)S(1)} all-reduce(f32[4,64,256]{2,1,0:T(8,128)} %reduce-scatter.2.cloned.1.call-done), channel_id=1, replica_groups=mesh['row'=4,'col'=2,'chan'=4] {'row','col'}, use_global_device_ids=true, to_apply=%region_1.2 | all-reduce | flops 65536 | bytes 393216 | tf_op jit(solution)/shard_map/psum | solution.py:508
  302.2 0.8 copy.60
  (7 shorter events, 0.2 us)
Async XLA Ops:
  8.9 89.3 %all-to-all-start = ((bf16[4,112,64]{1,2,0:T(8,128)(2,1)}), bf16[4,112,64]{1,2,0:T(8,128)(2,1)}, u32[]{:S(2)}, u32[]{:S(2)}) async-start(bf16[4,112,64]{1,2,0:T(8,128)(2,1)} %copy.51), calls=%async_computation | async-start | bytes 131072 | tf_op jit(solution)/shard_map/all_to_all | solution.py:491
  15.3 257.5 %reduce-scatter.2.cloned.1.call-start = ((), (), s32[]{:S(2)}) async-start(), calls=%async_computation.3 | async-start | bytes 1310720 | tf_op jit(solution)/shard_map/reduce_scatter | solution.py:507
  149.2 121.8 %all-to-all-start.1 = ((bf16[112,4,64]{0,2,1:T(8,128)(2,1)}), bf16[112,4,64]{0,2,1:T(8,128)(2,1)}, u32[]{:S(2)}, u32[]{:S(2)}) async-start(bf16[112,4,64]{0,2,1:T(8,128)(2,1)} %bitcast.12), calls=%async_computation.1 | async-start | bytes 131072 | tf_op jit(solution)/shard_map/all_to_all | solution.py:505
Sparse Core Ops, SparseCore 0:
  141.7 33.1 reduce-scatter.1

commit v2 on v1

--- a/solution.py
+++ b/solution.py
@@ -16,10 +16,6 @@
 LIMIT = 67_000_000
 
 
-def sigmoid(v):
-    return 1.0 / (1.0 + jnp.exp(-v))
-
-
 def silu_slope(values):
     logistic = jax.nn.sigmoid(values)
     return logistic * (1.0 + values * (1.0 - logistic))
@@ -40,8 +36,20 @@
     return cells.transpose(3, 1, 0, 2).reshape(count, tile_h, tile_w)
 
 
-def spread_kernel(n_row, n_col, x_ref, out_ref, local_sem, send_sems, recv_sems):
+def spread_kernel(n_row, n_col, n_chan, n_extra, summed, *refs):
+    x_ref, extras, refs = refs[0], refs[1 : 1 + n_extra], refs[1 + n_extra :]
+    if summed:
+        project_ref, refs = refs[0], refs[1:]
+    out_ref, gathered, refs = refs[0], refs[1 : 1 + n_extra], refs[1 + n_extra :]
+    if summed:
+        project_out, refs = refs[0], refs[1:]
+    local_sem, send_sems, recv_sems, extra_local, extra_send, extra_recv = refs[:6]
+    if summed:
+        stages, sum_local, sum_send, sum_recv = refs[6:13], refs[13], refs[14], refs[15]
     n_hi = n_row // 2
+    chan = lax.axis_index("chan")
+    chan_peer = [lax.rem(chan + d, n_chan) for d in range(n_chan)]
+    chan_from = [lax.rem(chan - d + n_chan, n_chan) for d in range(n_chan)]
     row = lax.axis_index("row")
     col = lax.axis_index("col")
     hi, core = row // 2, row % 2
@@ -57,6 +65,7 @@
     partners = [sibling]
     partners += [{"row": hi_peer[d] * 2 + core} for d in range(1, n_hi)]
     partners += [{"col": col_peer[d]} for d in range(1, n_col)]
+    partners += [{"chan": chan_peer[d]} for d in range(1, n_chan)]
 
     barrier = pltpu.get_barrier_semaphore()
     for who in partners:
@@ -119,10 +128,68 @@
             device_id_type=MESH,
         ).wait_recv()
 
+    later = []
+
+    def exchange(sources, landing, at, who, local, sends, recvs, base):
+        keep = pltpu.make_async_copy(sources[0], landing.at[at], local)
+        keep.start()
+        for d in range(1, len(sources)):
+            copy = pltpu.make_async_remote_copy(
+                src_ref=sources[d],
+                dst_ref=landing.at[at],
+                send_sem=sends.at[base + d - 1],
+                recv_sem=recvs.at[base + d - 1],
+                device_id=who[d],
+                device_id_type=MESH,
+            )
+            copy.start()
+            later.append(copy)
+
+        def finish(froms):
+            keep.wait()
+            for d in range(1, len(sources)):
+                pltpu.make_async_remote_copy(
+                    src_ref=landing.at[froms[d]],
+                    dst_ref=landing.at[froms[d]],
+                    send_sem=sends.at[base + d - 1],
+                    recv_sem=recvs.at[base + d - 1],
+                    device_id=who[d],
+                    device_id_type=MESH,
+                ).wait_recv()
+
+        return finish
+
+    chan_who = [{"chan": chan_peer[d]} for d in range(n_chan)]
     for d in range(1, n_hi):
         send(0, 0, 0, {"row": hi_peer[d] * 2 + core}, slot_of(0, d, 0, 0))
     for d in range(1, n_col):
         send(1, 0, 0, {"col": col_peer[d]}, slot_of(1, 0, d, 0))
+    if summed:
+        slab = project_ref.shape[1] // n_chan
+        slabs = [
+            project_ref.at[:, pl.ds(pl.multiple_of(chan_peer[d] * slab, 8), slab), :]
+            for d in range(n_chan)
+        ]
+        finish_sum = exchange(
+            slabs, stages[0], chan, chan_who, sum_local.at[0], sum_send, sum_recv, 0
+        )
+        hi_who = [{"row": hi_peer[d] * 2 + core} for d in range(n_hi)]
+        col_who = [{"col": col_peer[d]} for d in range(n_col)]
+        core_who = [sibling, sibling]
+
+    def total_of(stage, count):
+        value = stage[0].astype(jnp.float32)
+        for i in range(1, count):
+            value = value + stage[i].astype(jnp.float32)
+        return value
+
+    finish_extras = [
+        exchange(
+            [extras[i]] * n_chan, gathered[i], chan, chan_who,
+            extra_local.at[i], extra_send, extra_recv, i * (n_chan - 1),
+        )
+        for i in range(n_extra)
+    ]
     for d in range(1, n_col):
         send(0, 0, 0, {"col": col_peer[d]}, slot_of(0, 0, d, 0))
     for d in range(1, n_hi):
@@ -152,47 +219,107 @@
         for d in range(1, n_hi):
             send(1, 0, dc, {"row": hi_peer[d] * 2 + core}, slot_of(1, d, dc, 0))
         send(1, 0, dc, sibling, slot_of(1, 0, dc, 1))
+    if summed:
+        finish_sum(chan_from)
+        ready = stages[4]
+        ready[...] = total_of(stages[0], n_chan).astype(ready.dtype)
+        finish_sum = exchange(
+            [ready] * n_hi, stages[1], hi, hi_who, sum_local.at[1], sum_send, sum_recv, n_chan - 1
+        )
     for dc in range(1, n_col):
         arrive(0, 0, dc, 0)
         send(0, 0, dc, sibling, slot_of(0, 0, dc, 1))
     for dh in range(1, n_hi):
         arrive(1, dh, 0, 0)
         send(1, dh, 0, sibling, slot_of(1, dh, 0, 1))
+    if summed:
+        finish_sum(hi_from)
+        ready = stages[5]
+        ready[...] = total_of(stages[1], n_hi).astype(ready.dtype)
+        finish_sum = exchange(
+            [ready] * n_col, stages[2], col, col_who, sum_local.at[2],
+            sum_send, sum_recv, n_chan + n_hi - 2,
+        )
     for h in range(2):
         for dh in range(1, n_hi):
             for dc in range(1, n_col):
                 arrive(h, dh, dc, 0)
                 send(h, dh, dc, sibling, slot_of(h, dh, dc, 1))
+    if summed:
+        finish_sum(col_from)
+        ready = stages[6]
+        ready[...] = total_of(stages[2], n_col)
+        finish_sum = exchange(
+            [ready] * 2, stages[3], core, core_who, sum_local.at[3],
+            sum_send, sum_recv, n_chan + n_hi + n_col - 3,
+        )
     for h in range(2):
         for dh in range(n_hi):
             for dc in range(n_col):
                 arrive(h, dh, dc, 1)
+    if summed:
+        finish_sum([core, 1 - core])
+        project_out[...] = total_of(stages[3], 2).astype(project_out.dtype)
+    for finish in finish_extras:
+        finish(chan_from)
+    for copy in later:
+        copy.wait_send()
     own.wait()
     for copy in sent:
         copy.wait_send()
 
 
-def spread(cells, collective_id):
-    n_row, n_col = lax.axis_size("row"), lax.axis_size("col")
+def spread(cells, extras, project, collective_id):
+    n_row, n_col, n_chan = (lax.axis_size(axis) for axis in ("row", "col", "chan"))
+    n_hi = n_row // 2
     runs, rows, width = cells.shape
-    tiles = n_row // 2 * n_col
+    tiles = n_hi * n_col
     shape = (runs * n_col + 2 * MARGIN_RUNS, rows * n_row + 2 * MARGIN_ROWS, width)
-    copies = 2 * ((n_row // 2 - 1) + (n_col - 1) * (n_row // 2) + tiles) + 2 * tiles
+    copies = 2 * ((n_hi - 1) + (n_col - 1) * n_hi + tiles) + 2 * tiles
+    vmem = pl.BlockSpec(memory_space=VMEM)
+    dma = pltpu.SemaphoreType.DMA
+    operands = [cells, *extras]
+    outs = [jax.ShapeDtypeStruct(shape, cells.dtype)]
+    outs += [jax.ShapeDtypeStruct((n_chan, *e.shape), e.dtype) for e in extras]
+    scratch = [
+        dma,
+        dma((copies,)),
+        dma((4 * tiles,)),
+        dma((len(extras),)),
+        dma((len(extras) * (n_chan - 1),)),
+        dma((len(extras) * (n_chan - 1),)),
+    ]
+    if project is not None:
+        slab = (project.shape[0], project.shape[1] // n_chan, project.shape[2])
+        operands.append(project)
+        outs.append(jax.ShapeDtypeStruct(slab, jnp.bfloat16))
+        peers = n_chan + n_hi + n_col - 2
+        scratch += [
+            VMEM((n_chan, *slab), jnp.float32),
+            VMEM((n_hi, *slab), jnp.bfloat16),
+            VMEM((n_col, *slab), jnp.bfloat16),
+            VMEM((2, *slab), jnp.float32),
+            VMEM(slab, jnp.bfloat16),
+            VMEM(slab, jnp.bfloat16),
+            VMEM(slab, jnp.float32),
+            dma((4,)),
+            dma((peers,)),
+            dma((peers,)),
+        ]
+    body = functools.partial(
+        spread_kernel, n_row, n_col, n_chan, len(extras), project is not None
+    )
     return pl.pallas_call(
-        functools.partial(spread_kernel, n_row, n_col),
-        out_shape=jax.ShapeDtypeStruct(shape, cells.dtype),
-        in_specs=[pl.BlockSpec(memory_space=VMEM)],
-        out_specs=pl.BlockSpec(memory_space=VMEM),
-        scratch_shapes=[
-            pltpu.SemaphoreType.DMA,
-            pltpu.SemaphoreType.DMA((copies,)),
-            pltpu.SemaphoreType.DMA((4 * tiles,)),
-        ],
+        body,
+        out_shape=tuple(outs),
+        in_specs=[vmem] * len(operands),
+        out_specs=(vmem,) * len(outs),
+        scratch_shapes=scratch,
         compiler_params=pltpu.CompilerParams(
             collective_id=collective_id, has_side_effects=True, vmem_limit_bytes=LIMIT
         ),
         name="spread_tiles",
-    )(cells)
+    )(*operands)
 
 
 def tap_of(t):
@@ -481,18 +608,23 @@
     padded = size * n_chan
     taps = dilated_weight.reshape(27, local_in, out_count)
 
-    spread_x = spread(to_runs(features), 0)
     vectors = jnp.concatenate([branch_gain, branch_shift, project_shift[:, None]], axis=1)
-    vectors = lax.all_gather(vectors, "chan", axis=0, tiled=True).T
-    gain, shift, pshift = vectors[:4], vectors[4:8], vectors[8:9]
-    pw = lax.all_gather(project_weight, "chan", axis=0, tiled=True).transpose(1, 0, 2)
     cot = to_runs(cotangent).reshape(used, local_out)
     cot = jnp.pad(cot, ((0, padded - used), (0, 0)))
-    cot = lax.all_to_all(cot, "chan", split_axis=0, concat_axis=1, tiled=True)
+    spread_x, vectors, pw, cot = spread(
+        to_runs(features), [vectors, project_weight.transpose(1, 0, 2), cot], None, 0
+    )
+    vectors = vectors.transpose(2, 0, 1).reshape(9, out_count)
+    gain, shift, pshift = vectors[:4], vectors[4:8], vectors[8:9]
+    pw = pw.transpose(1, 0, 2, 3).reshape(4, out_count, out_count)
+    cot = lax.dynamic_slice_in_dim(cot, me * size, size, axis=1)
+    cot = cot.transpose(1, 0, 2).reshape(size, out_count)
 
     part = forward(spread_x, point_weight, taps, runs, rows, padded)
     mixed_out, project, grads = middle(part, gain, shift, pw, pshift, cot)
-    spread_b = spread(grads[:used].reshape(runs, rows, 4 * out_count), 1)
+    spread_b, mixed_out, project = spread(
+        grads[:used].reshape(runs, rows, 4 * out_count), [mixed_out], project, 1
+    )
 
     total_runs, total_rows, _ = spread_x.shape
     inner = spread_x[MARGIN_RUNS:-MARGIN_RUNS, MARGIN_ROWS:-MARGIN_ROWS]
@@ -502,16 +634,14 @@
         xt, spread_b, point_weight, taps, runs, rows
     )
 
-    mixed_out = lax.all_to_all(mixed_out, "chan", split_axis=1, concat_axis=0, tiled=True)
-    mixed_out = from_runs(mixed_out[:used], tile_h, tile_w)
-    project = lax.psum_scatter(project, "chan", scatter_dimension=1, tiled=True)
-    project = lax.psum(project, ("row", "col")).astype(jnp.bfloat16).transpose(1, 0, 2)
+    mixed_out = lax.dynamic_slice_in_dim(mixed_out, me * local_out, local_out, axis=2)
+    mixed_out = from_runs(mixed_out.reshape(padded, local_out)[:used], tile_h, tile_w)
     return (
         mixed_out,
         from_runs(input_grad, tile_h, tile_w),
         dilated_grad.reshape(dilated_weight.shape),
         point_grad,
-        project,
+        project.transpose(1, 0, 2),
     )
 
 

time: 311 us -> 249 us (0.80)
  blocking collectives: 59.8 us -> 0 us
  Pallas kernels: 197 us -> 219 us
  starting transfers between devices: 16 us -> 0 us
  between operations: 14.1 us -> 0.75 us
  local copies, waits for them, and re-layouts: 21.7 us -> 27.2 us
    all_gather x2 -> x0, blocking collectives: 30.3 us -> none  [the longest x1 16.7 us: per_device(): lax.all_gather(project_weight, 'chan', axis=0, tiled=True)]
    psum x1 -> x0, blocking collectives: 29.5 us -> none  [per_device(): lax.psum(project, ('row', 'col')).astype(jnp.bfloat16).transpose(1, 0, 2)]
    pallas_call x2, Pallas kernels: 66.4 us -> 87.7 us  [spread(): pl.pallas_call(body, out_shape=tuple(outs), in_specs=[vmem] * len(operand...]
    all_to_all x2 -> x0, starting transfers between devices: 16 us -> none  [the longest x1 9.69 us: per_device(): lax.all_to_all(mixed_out, 'chan', split_axis=1, concat_axis=0, tiled=True)]
    all_to_all x4 -> x0, local copies, waits for them, and re-layouts: 3.29 us -> none  [the longest x2 2.29 us: per_device(): cot = lax.all_to_all(cot, 'chan', split_axis=0, concat_axis=1, tiled=True)]
  transfers between devices with their start and end apart: 3 -> 0, of which waited for: 0 -> 0; matrix products, arithmetic and copies ran while one was open for 6% -> 0% of each run, Pallas kernels for 50% -> 0%
where the time goes in v2:
time: 249 us; the launch traced here: 248 us
  Pallas kernels  219 us (88%)
  local copies, waits for them, and re-layouts  27.2 us (11%)
    pallas_call x2, Pallas kernels, spread(): pl.pallas_call(body, out_shape=tuple(outs), in_specs=[vmem] * len(operand...  87.7 us
    pallas_call x1, Pallas kernels, backward(): pl.pallas_call(functools.partial(backward_kernel, runs, rows), grid=(28,)...  65.9 us
    pallas_call x1, Pallas kernels, middle(): pl.pallas_call(functools.partial(middle_kernel, n_chan), out_shape=(jax.S...  42.3 us
    pallas_call x1, Pallas kernels, forward(): pl.pallas_call(functools.partial(forward_kernel, runs, rows), grid=(28,),...  23.3 us

profile of v2, /device:TPU:0, one launch (start us, length us, event | category | flops | bytes accessed | tf_op | source)
XLA Modules:
  0.0 247.9 jit_solution(9725601948882810966)
XLA Ops:
  0.6 0.7 pad_maximum_fusion
  1.4 0.7 copy.58.refs_1_
  2.1 0.9 reshape.58
  3.1 0.7 pad.14.refs_3_
  3.8 1.6 copy.74
  5.3 1.1 reshape.56
  6.5 0.8 pad_bitcast_fusion.refs_0_
  7.3 34.5 %spread_tiles.2 = (bf16[12,864,512]{2,1,0:T(8,128)(2,1)}, f32[4,64,9]{2,1,0:T(8,128)}, bf16[4,4,64,256]{3,2,1,0:T(8,128)(2,1)}, bf16[4,448,64]{2,1,0:T(8,128)(2,1)}) custom-call(bf16[3,144,512]{2,1,0:T(8,128)(2,1)} %pad_bitcast_fusion.refs_0_, f32[64,9]{1,0:T(8,128)} %copy.58.refs_1_, bf16[4,64,256]{2,1,0:T(8,128)(2,1)} %bitcast.48, bf16[448,64]{1,0:T(8,128)(2,1)} %pad.14.refs_3_), custom_call_target="tpu_custom_call" | custom-call | tf_op jit(solution)/shard_map/spread_tiles/pallas_call | solution.py:312
  41.8 1.9 copy.61
  43.7 1.1 slice_reduce_fusion
  44.8 0.7 slice.38.pshift_ref
  45.4 0.9 dynamic-slice_bitcast_fusion
  46.4 0.1 copy.62
  46.5 0.7 copy.63.cot_ref
  47.2 1.1 fusion
  48.3 0.7 copy.70.shift_ref
  49.0 0.7 copy.69.gain_ref
  49.6 23.3 %forward_taps.1.part_ref = bf16[4,448,256]{2,1,0:T(8,128)(2,1)} custom-call(bf16[12,864,512]{2,1,0:T(8,128)(2,1)} %get-tuple-element.18.x_ref, bf16[512,256]{1,0:T(8,128)(2,1)} %wp_ref.3, bf16[27,512,256]{2,1,0:T(8,128)(2,1)} %bitcast.39), custom_call_target="tpu_custom_call" | custom-call | tf_op jit(solution)/shard_map/forward_taps/pallas_call | solution.py:367
  72.9 2.2 slice.42
  75.2 3.8 %copy.65 = bf16[3,1152,512]{1,2,0:T(8,128)(2,1)} copy(bf16[3,1152,512]{2,1,0:T(8,128)(2,1)S(1)} %bitcast.41) | data formatting | bytes 7077888 | tf_op jit(solution)/shard_map/reshape | solution.py:632
  78.9 42.3 %middle.1 = (bf16[112,256]{1,0:T(8,128)(2,1)}, f32[4,256,256]{2,1,0:T(8,128)}, bf16[448,1024]{1,0:T(8,128)(2,1)}) custom-call(bf16[4,448,256]{2,1,0:T(8,128)(2,1)} %forward_taps.1.part_ref, f32[4,256]{1,0:T(4,128)} %copy.69.gain_ref, f32[4,256]{1,0:T(4,128)} %copy.70.shift_ref, bf16[4,256,256]{2,1,0:T(8,128)(2,1)} %bitcast.44, f32[1,256]{1,0:T(1,128)} %slice.38.pshift_ref, ...), custom_call_target="tpu_custom_call" | custom-call | tf_op jit(solution)/shard_map/middle/pallas_call | solution.py:477
  121.2 2.1 slice.39
  123.4 53.3 %spread_tiles.3 = (bf16[12,864,1024]{2,1,0:T(8,128)(2,1)}, bf16[4,112,256]{2,1,0:T(8,128)(2,1)}, bf16[4,64,256]{2,1,0:T(8,128)(2,1)}) custom-call(bf16[3,144,1024]{2,1,0:T(8,128)(2,1)} %bitcast.43, bf16[112,256]{1,0:T(8,128)(2,1)} %get-tuple-element.23.refs_1_, f32[4,256,256]{2,1,0:T(8,128)} %get-tuple-element.24.refs_2_), custom_call_target="tpu_custom_call" | custom-call | tf_op jit(solution)/shard_map/spread_tiles/pallas_call | solution.py:312
  176.6 1.0 constant_dynamic-slice_fusion
  177.7 0.7 copy.67
  178.4 1.7 copy.68
  180.0 65.9 %backward_taps.1 = (bf16[512,256]{1,0:T(8,128)(2,1)}, bf16[27,512,256]{2,1,0:T(8,128)(2,1)}, bf16[432,512]{1,0:T(8,128)(2,1)}) custom-call(bf16[3,512,1152]{2,1,0:T(8,128)(2,1)} %bitcast.42, bf16[12,864,1024]{2,1,0:T(8,128)(2,1)} %get-tuple-element.26.b_ref, bf16[512,256]{1,0:T(8,128)(2,1)} %wp_ref.3, bf16[27,512,256]{2,1,0:T(8,128)(2,1)} %bitcast.40), custom_call_target="tpu_custom_call" | custom-call | tf_op jit(solution)/shard_map/backward_taps/pallas_call | solution.py:560
  245.9 1.0 slice_bitcast_fusion
  247.0 0.9 reshape.68
  (6 shorter events, 0.1 us)

commit v3 on v2

--- a/solution.py
+++ b/solution.py
@@ -496,42 +496,64 @@
     )(part, gain, shift, pw, pshift, cot)
 
 
-def backward_kernel(runs, rows, xt_ref, b_ref, wp_ref, w_ref, point_ref, dil_ref, in_ref, total, grad):
+def backward_kernel(
+    runs, rows, xt_ref, b_ref, wp_ref, w_ref, in_ref, dil_ref,
+    total, grad, held, keep_sems, send_sems, recv_sems,
+):
     t = pl.program_id(0)
     branch, down, across = tap_of(t)
-    pairs, width, depth = xt_ref.shape
+    pairs, half, depth = xt_ref.shape
     out_count = b_ref.shape[-1]
     full_rows = b_ref.shape[1] - 2 * MARGIN_ROWS
     y_off = pl.multiple_of(MARGIN_ROWS - down * (RATE_STEP * SLOT), 16)
-
-    def step(g, _):
+    row = lax.axis_index("row")
+    core = row % 2
+    sibling = {"row": row - core + 1 - core}
+    mine = pl.ds(pl.multiple_of(core * half, 16), half)
+    other = pl.ds(pl.multiple_of((1 - core) * half, 16), half)
+
+    @pl.when(t == 0)
+    def _():
+        barrier = pltpu.get_barrier_semaphore()
+        pl.semaphore_signal(barrier, inc=1, device_id=sibling, device_id_type=MESH)
+        pl.semaphore_wait(barrier, 1)
+
+    def moves(step, slot):
+        keep = pltpu.make_async_copy(held.at[slot], dil_ref.at[step, mine, :], keep_sems.at[slot])
+        give = pltpu.make_async_remote_copy(
+            src_ref=held.at[slot],
+            dst_ref=dil_ref.at[step, mine, :],
+            send_sem=send_sems.at[slot],
+            recv_sem=recv_sems.at[step],
+            device_id=sibling,
+            device_id_type=MESH,
+        )
+        return keep, give
+
+    slot = lax.rem(t, 2)
+    for g in range(pairs):
         cells = b_ref[pl.ds(MARGIN_RUNS - across + 2 * g, 2), pl.ds(y_off, full_rows), :]
         part = jnp.dot(
             xt_ref[g], cells.reshape(depth, out_count), preferred_element_type=jnp.float32
         )
-
-        @pl.when(g == 0)
-        def _():
+        if g == 0:
             grad[...] = part
-
-        @pl.when(g > 0)
-        def _():
+        else:
             grad[...] += part
 
-        return 0
-
-    lax.fori_loop(0, pairs, step, 0)
-
-    @pl.when(t == 0)
+    @pl.when(t >= 2)
     def _():
-        point_ref[...] = grad[...].astype(jnp.bfloat16)
-
-    @pl.when(t > 0)
-    def _():
-        dil_ref[0] = grad[...].astype(jnp.bfloat16)
+        keep, give = moves(t - 2, slot)
+        keep.wait()
+        give.wait_send()
+
+    held[slot] = grad[...].astype(jnp.bfloat16)
+    keep, give = moves(t, slot)
+    keep.start()
+    give.start()
 
     u0 = MARGIN_RUNS + runs * lax.axis_index("col") - across
-    y0 = MARGIN_ROWS + rows * lax.axis_index("row") - down * (RATE_STEP * SLOT)
+    y0 = MARGIN_ROWS + rows * row - down * (RATE_STEP * SLOT)
     window = b_ref[pl.ds(u0, runs), pl.ds(pl.multiple_of(y0, 16), rows), :].reshape(
         runs * rows, out_count
     )
@@ -551,19 +573,37 @@
     @pl.when(t == 27)
     def _():
         in_ref[...] = total[...].astype(jnp.bfloat16)
+        for step in (26, 27):
+            keep, give = moves(step, step % 2)
+            keep.wait()
+            give.wait_send()
+
+        def landed(step, _):
+            there = dil_ref.at[step, other, :]
+            pltpu.make_async_remote_copy(
+                src_ref=there,
+                dst_ref=there,
+                send_sem=send_sems.at[0],
+                recv_sem=recv_sems.at[step],
+                device_id=sibling,
+                device_id_type=MESH,
+            ).wait_recv()
+            return 0
+
+        lax.fori_loop(0, 28, landed, 0)
 
 
 def backward(xt, spread_b, point_weight, taps, runs, rows):
     width, out_count = point_weight.shape
     total_runs, total_rows, _ = spread_b.shape
+    half = width // 2
     tap_index = lambda t: (jnp.maximum(t - 1, 0), 0, 0)
     return pl.pallas_call(
         functools.partial(backward_kernel, runs, rows),
         grid=(28,),
         out_shape=(
-            jax.ShapeDtypeStruct((width, out_count), jnp.bfloat16),
-            jax.ShapeDtypeStruct((27, width, out_count), jnp.bfloat16),
             jax.ShapeDtypeStruct((runs * rows, width), jnp.bfloat16),
+            jax.ShapeDtypeStruct((28, width, out_count), jnp.bfloat16),
         ),
         in_specs=[
             pl.BlockSpec(memory_space=VMEM),
@@ -572,16 +612,22 @@
             pl.BlockSpec((1, width, out_count), tap_index),
         ],
         out_specs=(
-            pl.BlockSpec((width, out_count), lambda t: (0, 0)),
-            pl.BlockSpec((1, width, out_count), tap_index),
             pl.BlockSpec((runs * rows, width), lambda t: (0, 0)),
+            pl.BlockSpec(memory_space=pl.ANY),
         ),
         scratch_shapes=[
             VMEM((runs * rows, width), jnp.float32),
-            VMEM((width, out_count), jnp.float32),
+            VMEM((half, out_count), jnp.float32),
+            VMEM((2, half, out_count), jnp.bfloat16),
+            pltpu.SemaphoreType.DMA((2,)),
+            pltpu.SemaphoreType.DMA((2,)),
+            pltpu.SemaphoreType.DMA((28,)),
         ],
         compiler_params=pltpu.CompilerParams(
-            dimension_semantics=("arbitrary",), vmem_limit_bytes=LIMIT
+            dimension_semantics=("arbitrary",),
+            vmem_limit_bytes=LIMIT,
+            collective_id=3,
+            has_side_effects=True,
         ),
         name="backward_taps",
     )(xt, spread_b, point_weight, taps)
@@ -629,8 +675,10 @@
     total_runs, total_rows, _ = spread_x.shape
     inner = spread_x[MARGIN_RUNS:-MARGIN_RUNS, MARGIN_ROWS:-MARGIN_ROWS]
     pairs = inner.shape[0] // 2
-    xt = inner.reshape(pairs, 2 * inner.shape[1], local_in).transpose(0, 2, 1)
-    point_grad, dilated_grad, input_grad = backward(
+    half = local_in // 2
+    inner = lax.dynamic_slice_in_dim(inner, lax.axis_index("row") % 2 * half, half, axis=2)
+    xt = inner.reshape(pairs, 2 * inner.shape[1], half).transpose(0, 2, 1)
+    input_grad, weight_grads = backward(
         xt, spread_b, point_weight, taps, runs, rows
     )
 
@@ -639,8 +687,8 @@
     return (
         mixed_out,
         from_runs(input_grad, tile_h, tile_w),
-        dilated_grad.reshape(dilated_weight.shape),
-        point_grad,
+        weight_grads[1:].reshape(dilated_weight.shape),
+        weight_grads[0],
         project.transpose(1, 0, 2),
     )
 

time: 249 us -> 237 us (0.952)
  Pallas kernels: 219 us -> 200 us
  local copies, waits for them, and re-layouts: 27.2 us -> 34.2 us
    pallas_call x1, Pallas kernels: 65.9 us -> 46.6 us  [backward(): pl.pallas_call(functools.partial(backward_kernel, runs, rows), grid=(28,)...]
    slice x0 -> x1, local copies, waits for them, and re-layouts: none -> 6.73 us  [per_device(): weight_grads[1:].reshape(dilated_weight.shape)]
where the time goes in v3:
time: 237 us; the launch traced here: 236 us
  Pallas kernels  200 us (84%)
  local copies, waits for them, and re-layouts  34.2 us (14%)
    pallas_call x2, Pallas kernels, spread(): pl.pallas_call(body, out_shape=tuple(outs), in_specs=[vmem] * len(operand...  87.8 us
    pallas_call x1, Pallas kernels, backward(): pl.pallas_call(functools.partial(backward_kernel, runs, rows), grid=(28,)...  46.6 us
    pallas_call x1, Pallas kernels, middle(): pl.pallas_call(functools.partial(middle_kernel, n_chan), out_shape=(jax.S...  42.2 us
    pallas_call x1, Pallas kernels, forward(): pl.pallas_call(functools.partial(forward_kernel, runs, rows), grid=(28,),...  23.3 us
    slice x1, local copies, waits for them, and re-layouts, per_device(): weight_grads[1:].reshape(dilated_weight.shape)  6.73 us

profile of v3, /device:TPU:0, one launch (start us, length us, event | category | flops | bytes accessed | tf_op | source)
XLA Modules:
  0.0 235.6 jit_solution(437734512772840942)
XLA Ops:
  0.6 0.7 pad_maximum_fusion
  1.4 0.7 copy.58.refs_1_
  2.1 0.9 reshape.58
  3.1 0.7 pad.14.refs_3_
  3.8 1.6 copy.74
  5.3 1.1 reshape.56
  6.5 0.8 pad_bitcast_fusion.refs_0_
  7.3 34.6 %spread_tiles.2 = (bf16[12,864,512]{2,1,0:T(8,128)(2,1)}, f32[4,64,9]{2,1,0:T(8,128)}, bf16[4,4,64,256]{3,2,1,0:T(8,128)(2,1)}, bf16[4,448,64]{2,1,0:T(8,128)(2,1)}) custom-call(bf16[3,144,512]{2,1,0:T(8,128)(2,1)} %pad_bitcast_fusion.refs_0_, f32[64,9]{1,0:T(8,128)} %copy.58.refs_1_, bf16[4,64,256]{2,1,0:T(8,128)(2,1)} %bitcast.51, bf16[448,64]{1,0:T(8,128)(2,1)} %pad.14.refs_3_), custom_call_target="tpu_custom_call" | custom-call | tf_op jit(solution)/shard_map/spread_tiles/pallas_call | solution.py:312
  41.9 1.9 copy.61
  43.8 1.1 slice_reduce_fusion
  44.9 0.7 slice.44.pshift_ref
  45.6 0.9 dynamic-slice_bitcast_fusion
  46.5 0.1 copy.62
  46.6 0.7 copy.63.cot_ref
  47.3 1.1 fusion
  48.4 0.7 copy.70.shift_ref
  49.1 0.7 copy.69.gain_ref
  49.8 23.3 %forward_taps.1.part_ref = bf16[4,448,256]{2,1,0:T(8,128)(2,1)} custom-call(bf16[12,864,512]{2,1,0:T(8,128)(2,1)} %get-tuple-element.17.x_ref, bf16[512,256]{1,0:T(8,128)(2,1)} %wp_ref.3, bf16[27,512,256]{2,1,0:T(8,128)(2,1)} %bitcast.41), custom_call_target="tpu_custom_call" | custom-call | tf_op jit(solution)/shard_map/forward_taps/pallas_call | solution.py:367
  73.1 2.2 slice.48
  75.3 0.1 constant_dynamic-slice_fusion
  75.5 2.2 copy.65
  77.7 42.2 %middle.1 = (bf16[112,256]{1,0:T(8,128)(2,1)}, f32[4,256,256]{2,1,0:T(8,128)}, bf16[448,1024]{1,0:T(8,128)(2,1)}) custom-call(bf16[4,448,256]{2,1,0:T(8,128)(2,1)} %forward_taps.1.part_ref, f32[4,256]{1,0:T(4,128)} %copy.69.gain_ref, f32[4,256]{1,0:T(4,128)} %copy.70.shift_ref, bf16[4,256,256]{2,1,0:T(8,128)(2,1)} %bitcast.47, f32[1,256]{1,0:T(1,128)} %slice.44.pshift_ref, ...), custom_call_target="tpu_custom_call" | custom-call | tf_op jit(solution)/shard_map/middle/pallas_call | solution.py:477
  119.9 2.2 slice.45
  122.1 53.2 %spread_tiles.3 = (bf16[12,864,1024]{2,1,0:T(8,128)(2,1)}, bf16[4,112,256]{2,1,0:T(8,128)(2,1)}, bf16[4,64,256]{2,1,0:T(8,128)(2,1)}) custom-call(bf16[3,144,1024]{2,1,0:T(8,128)(2,1)} %bitcast.46, bf16[112,256]{1,0:T(8,128)(2,1)} %get-tuple-element.22.refs_1_, f32[4,256,256]{2,1,0:T(8,128)} %get-tuple-element.23.refs_2_), custom_call_target="tpu_custom_call" | custom-call | tf_op jit(solution)/shard_map/spread_tiles/pallas_call | solution.py:312
  175.3 1.0 constant_dynamic-slice_fusion.1
  176.3 0.7 copy.67
  177.0 1.7 copy.68
  178.7 46.6 %backward_taps.1 = (bf16[432,512]{1,0:T(8,128)(2,1)}, bf16[28,512,256]{2,1,0:T(8,128)(2,1)}) custom-call(bf16[3,256,1152]{2,1,0:T(8,128)(2,1)} %bitcast.45, bf16[12,864,1024]{2,1,0:T(8,128)(2,1)} %get-tuple-element.25.b_ref, bf16[512,256]{1,0:T(8,128)(2,1)} %wp_ref.3, bf16[27,512,256]{2,1,0:T(8,128)(2,1)} %bitcast.42), custom_call_target="tpu_custom_call" | custom-call | tf_op jit(solution)/shard_map/backward_taps/pallas_call | solution.py:601
  225.2 1.0 slice_bitcast_fusion
  226.3 0.9 reshape.68
  227.2 1.7 slice_bitcast_fusion.1
  228.9 6.7 %slice.50 = bf16[27,512,256]{2,1,0:T(8,128)(2,1)} slice(bf16[28,512,256]{2,1,0:T(8,128)(2,1)} %get-tuple-element.27), slice={[1:28], [0:512], [0:256]} | slice | bytes 14155776 | tf_op jit(solution)/shard_map/slice | solution.py:690
  (6 shorter events, 0.1 us)

commit v4 on v3

--- a/solution.py
+++ b/solution.py
@@ -331,8 +331,40 @@
     return branch, down, across
 
 
-def forward_kernel(runs, rows, x_ref, wp_ref, w_ref, out_ref, total):
+def forward_kernel(
+    runs, rows, n_chan, x_ref, wp_ref, w_ref, out_ref,
+    total, held, landed, send_sems, recv_sems, local_sems,
+):
     t = pl.program_id(0)
+    me = lax.axis_index("chan")
+    size = out_ref.shape[1]
+    peers = [lax.rem(me + d, n_chan) for d in range(n_chan)]
+
+    @pl.when(t == 0)
+    def _():
+        barrier = pltpu.get_barrier_semaphore()
+        for d in range(1, n_chan):
+            pl.semaphore_signal(
+                barrier, inc=1, device_id={"chan": peers[d]}, device_id_type=MESH
+            )
+        pl.semaphore_wait(barrier, n_chan - 1)
+
+    def share(b, d):
+        return held.at[b, pl.ds(pl.multiple_of(peers[d] * size, 16), size), :]
+
+    def keep(b):
+        return pltpu.make_async_copy(share(b, 0), landed.at[0, b], local_sems.at[b])
+
+    def give(b, d):
+        return pltpu.make_async_remote_copy(
+            src_ref=share(b, d),
+            dst_ref=landed.at[d, b],
+            send_sem=send_sems.at[b, d],
+            recv_sem=recv_sems.at[b, d],
+            device_id={"chan": peers[d]},
+            device_id_type=MESH,
+        )
+
     branch, down, across = tap_of(t)
     u0 = MARGIN_RUNS + runs * lax.axis_index("col") + across
     y0 = MARGIN_ROWS + rows * lax.axis_index("row") + down * (RATE_STEP * SLOT)
@@ -352,31 +384,58 @@
     def _():
         total[...] += part
 
-    @pl.when(lax.rem(t, 9) == 0)
-    def _():
-        used = runs * rows
-        out_ref[0, pl.ds(0, used), :] = total[...].astype(out_ref.dtype)
-        if out_ref.shape[1] > used:
-            out_ref[0, pl.ds(used, out_ref.shape[1] - used), :] = jnp.zeros(
-                (out_ref.shape[1] - used, out_ref.shape[2]), out_ref.dtype
-            )
-
-
-def forward(spread_x, point_weight, taps, runs, rows, padded):
+    used = runs * rows
+    for b in range(4):
+
+        @pl.when(t == 9 * b)
+        def _():
+            held[b, pl.ds(0, used), :] = total[...].astype(held.dtype)
+            if held.shape[1] > used:
+                held[b, pl.ds(used, held.shape[1] - used), :] = jnp.zeros(
+                    (held.shape[1] - used, held.shape[2]), held.dtype
+                )
+            keep(b).start()
+            for d in range(1, n_chan):
+                give(b, d).start()
+
+    @pl.when(t == 27)
+    def _():
+        for b in range(4):
+            keep(b).wait()
+            for d in range(1, n_chan):
+                give(b, d).wait()
+            pre = landed[0, b].astype(jnp.float32)
+            for d in range(1, n_chan):
+                pre = pre + landed[d, b].astype(jnp.float32)
+            out_ref[b] = pre
+
+
+def forward(spread_x, point_weight, taps, runs, rows, size):
     width, out_count = point_weight.shape
+    n_chan = lax.axis_size("chan")
     return pl.pallas_call(
-        functools.partial(forward_kernel, runs, rows),
+        functools.partial(forward_kernel, runs, rows, n_chan),
         grid=(28,),
-        out_shape=jax.ShapeDtypeStruct((4, padded, out_count), jnp.bfloat16),
+        out_shape=jax.ShapeDtypeStruct((4, size, out_count), jnp.float32),
         in_specs=[
             pl.BlockSpec(memory_space=VMEM),
             pl.BlockSpec(memory_space=VMEM),
             pl.BlockSpec((1, width, out_count), lambda t: (jnp.maximum(t - 1, 0), 0, 0)),
         ],
-        out_specs=pl.BlockSpec((1, padded, out_count), lambda t: ((t + 8) // 9, 0, 0)),
-        scratch_shapes=[VMEM((runs * rows, out_count), jnp.float32)],
+        out_specs=pl.BlockSpec((4, size, out_count), lambda t: (0, 0, 0)),
+        scratch_shapes=[
+            VMEM((runs * rows, out_count), jnp.float32),
+            VMEM((4, size * n_chan, out_count), jnp.bfloat16),
+            VMEM((n_chan, 4, size, out_count), jnp.bfloat16),
+            pltpu.SemaphoreType.DMA((4, n_chan)),
+            pltpu.SemaphoreType.DMA((4, n_chan)),
+            pltpu.SemaphoreType.DMA((4,)),
+        ],
         compiler_params=pltpu.CompilerParams(
-            dimension_semantics=("arbitrary",), vmem_limit_bytes=LIMIT
+            dimension_semantics=("arbitrary",),
+            vmem_limit_bytes=LIMIT,
+            collective_id=4,
+            has_side_effects=True,
         ),
         name="forward_taps",
     )(spread_x, point_weight, taps)
@@ -384,7 +443,7 @@
 
 def middle_kernel(
     n_chan, part_ref, gain_ref, shift_ref, pw_ref, pshift_ref, cot_ref,
-    out_ref, project_ref, grad_ref, landed, own, send_sems, recv_sems, send2, recv2, local_sem,
+    out_ref, project_ref, grad_ref, own, send2, recv2, local_sem,
 ):
     me = lax.axis_index("chan")
     size = cot_ref.shape[0]
@@ -395,29 +454,12 @@
     for d in range(1, n_chan):
         pl.semaphore_signal(barrier, inc=1, device_id={"chan": peers[d]}, device_id_type=MESH)
     pl.semaphore_wait(barrier, n_chan - 1)
-    copies = []
-    for d in range(1, n_chan):
-        copy = pltpu.make_async_remote_copy(
-            src_ref=part_ref.at[:, pl.ds(pl.multiple_of(peers[d] * size, 16), size), :],
-            dst_ref=landed.at[d - 1],
-            send_sem=send_sems.at[d - 1],
-            recv_sem=recv_sems.at[d - 1],
-            device_id={"chan": peers[d]},
-            device_id_type=MESH,
-        )
-        copy.start()
-        copies.append(copy)
-    for copy in copies:
-        copy.wait_recv()
     acts = []
     mixed = jnp.zeros((size, width), jnp.float32)
     hiddens = []
     mine = pl.ds(pl.multiple_of(me * size, 16), size)
     for b in range(4):
-        pre = part_ref[b, mine, :].astype(jnp.float32)
-        for d in range(n_chan - 1):
-            pre = pre + landed[d, b].astype(jnp.float32)
-        act = pre * gain_ref[b][None, :] + shift_ref[b][None, :]
+        act = part_ref[b] * gain_ref[b][None, :] + shift_ref[b][None, :]
         hidden = (act * jax.nn.sigmoid(act)).astype(jnp.bfloat16)
         acts.append(act)
         hiddens.append(hidden)
@@ -465,7 +507,7 @@
             device_id={"chan": peers[d]},
             device_id_type=MESH,
         ).wait_recv()
-    for copy in copies + grads:
+    for copy in grads:
         copy.wait_send()
 
 
@@ -484,9 +526,8 @@
         in_specs=[vmem] * 6,
         out_specs=(vmem,) * 3,
         scratch_shapes=[
-            VMEM((n_chan - 1, 4, size, width), jnp.bfloat16),
             VMEM((size, 4 * width), jnp.bfloat16),
-            dma, dma, dma, dma,
+            dma, dma,
             pltpu.SemaphoreType.DMA,
         ],
         compiler_params=pltpu.CompilerParams(
@@ -666,7 +707,7 @@
     cot = lax.dynamic_slice_in_dim(cot, me * size, size, axis=1)
     cot = cot.transpose(1, 0, 2).reshape(size, out_count)
 
-    part = forward(spread_x, point_weight, taps, runs, rows, padded)
+    part = forward(spread_x, point_weight, taps, runs, rows, size)
     mixed_out, project, grads = middle(part, gain, shift, pw, pshift, cot)
     spread_b, mixed_out, project = spread(
         grads[:used].reshape(runs, rows, 4 * out_count), [mixed_out], project, 1

time: 237 us -> 222 us (0.937)
  Pallas kernels: 200 us -> 185 us
    pallas_call x1, Pallas kernels: 42.2 us -> 21.5 us  [middle(): pl.pallas_call(functools.partial(middle_kernel, n_chan), out_shape=(jax.S...]
    pallas_call x1, Pallas kernels: 23.3 us -> 31.6 us  [forward(): pl.pallas_call(functools.partial(forward_kernel, runs, rows, n_chan), gri...]
where the time goes in v4:
time: 222 us; the launch traced here: 221 us
  Pallas kernels  185 us (83%)
  local copies, waits for them, and re-layouts  34.2 us (15%)
    pallas_call x2, Pallas kernels, spread(): pl.pallas_call(body, out_shape=tuple(outs), in_specs=[vmem] * len(operand...  85.4 us
    pallas_call x1, Pallas kernels, backward(): pl.pallas_call(functools.partial(backward_kernel, runs, rows), grid=(28,)...  46.6 us
    pallas_call x1, Pallas kernels, forward(): pl.pallas_call(functools.partial(forward_kernel, runs, rows, n_chan), gri...  31.6 us
    pallas_call x1, Pallas kernels, middle(): pl.pallas_call(functools.partial(middle_kernel, n_chan), out_shape=(jax.S...  21.5 us
    slice x1, local copies, waits for them, and re-layouts, per_device(): weight_grads[1:].reshape(dilated_weight.shape)  6.73 us

profile of v4, /device:TPU:0, one launch (start us, length us, event | category | flops | bytes accessed | tf_op | source)
XLA Modules:
  0.0 220.8 jit_solution(10981365818170827740)
XLA Ops:
  0.6 0.7 pad_maximum_fusion
  1.4 0.7 copy.58.refs_1_
  2.1 0.9 reshape.58
  3.1 0.7 pad.14.refs_3_
  3.8 1.6 copy.74
  5.3 1.1 reshape.56
  6.5 0.8 pad_bitcast_fusion.refs_0_
  7.3 34.5 %spread_tiles.2 = (bf16[12,864,512]{2,1,0:T(8,128)(2,1)}, f32[4,64,9]{2,1,0:T(8,128)}, bf16[4,4,64,256]{3,2,1,0:T(8,128)(2,1)}, bf16[4,448,64]{2,1,0:T(8,128)(2,1)}) custom-call(bf16[3,144,512]{2,1,0:T(8,128)(2,1)} %pad_bitcast_fusion.refs_0_, f32[64,9]{1,0:T(8,128)} %copy.58.refs_1_, bf16[4,64,256]{2,1,0:T(8,128)(2,1)} %bitcast.51, bf16[448,64]{1,0:T(8,128)(2,1)} %pad.14.refs_3_), custom_call_target="tpu_custom_call" | custom-call | tf_op jit(solution)/shard_map/spread_tiles/pallas_call | solution.py:312
  41.8 1.9 copy.61
  43.7 1.1 slice_reduce_fusion
  44.8 0.7 slice.44.pshift_ref
  45.5 0.9 dynamic-slice_bitcast_fusion
  46.4 0.1 copy.62
  46.5 0.7 copy.63.cot_ref
  47.2 1.1 fusion
  48.3 0.7 copy.70.shift_ref
  49.0 0.7 copy.69.gain_ref
  49.6 31.6 %forward_taps.1.part_ref = f32[4,112,256]{2,1,0:T(8,128)} custom-call(bf16[12,864,512]{2,1,0:T(8,128)(2,1)} %get-tuple-element.17.x_ref, bf16[512,256]{1,0:T(8,128)(2,1)} %wp_ref.3, bf16[27,512,256]{2,1,0:T(8,128)(2,1)} %bitcast.41), custom_call_target="tpu_custom_call" | custom-call | tf_op jit(solution)/shard_map/forward_taps/pallas_call | solution.py:416
  81.2 2.2 %slice.48 = bf16[6,576,512]{2,1,0:T(8,128)(2,1)S(1)} slice(bf16[12,864,512]{2,1,0:T(8,128)(2,1)} %get-tuple-element.17.x_ref), slice={[3:9], [144:720], [0:512]} | slice | bytes 7077888 | tf_op jit(solution)/shard_map/slice | solution.py:717
  83.5 0.1 constant_dynamic-slice_fusion
  83.6 2.2 %copy.65 = bf16[3,1152,256]{1,2,0:T(8,128)(2,1)} copy(bf16[3,1152,256]{2,1,0:T(8,128)(2,1)S(1)} %bitcast.44) | data formatting | bytes 3538944 | tf_op jit(solution)/shard_map/reshape | solution.py:721
  85.8 21.5 %middle.1 = (bf16[112,256]{1,0:T(8,128)(2,1)}, f32[4,256,256]{2,1,0:T(8,128)}, bf16[448,1024]{1,0:T(8,128)(2,1)}) custom-call(f32[4,112,256]{2,1,0:T(8,128)} %forward_taps.1.part_ref, f32[4,256]{1,0:T(4,128)} %copy.69.gain_ref, f32[4,256]{1,0:T(4,128)} %copy.70.shift_ref, bf16[4,256,256]{2,1,0:T(8,128)(2,1)} %bitcast.47, f32[1,256]{1,0:T(1,128)} %slice.44.pshift_ref, ...), custom_call_target="tpu_custom_call" | custom-call | tf_op jit(solution)/shard_map/middle/pallas_call | solution.py:519
  107.3 2.2 slice.45
  109.5 51.0 %spread_tiles.3 = (bf16[12,864,1024]{2,1,0:T(8,128)(2,1)}, bf16[4,112,256]{2,1,0:T(8,128)(2,1)}, bf16[4,64,256]{2,1,0:T(8,128)(2,1)}) custom-call(bf16[3,144,1024]{2,1,0:T(8,128)(2,1)} %bitcast.46, bf16[112,256]{1,0:T(8,128)(2,1)} %get-tuple-element.22.refs_1_, f32[4,256,256]{2,1,0:T(8,128)} %get-tuple-element.23.refs_2_), custom_call_target="tpu_custom_call" | custom-call | tf_op jit(solution)/shard_map/spread_tiles/pallas_call | solution.py:312
  160.5 1.0 constant_dynamic-slice_fusion.1
  161.5 0.7 copy.67
  162.2 1.7 copy.68
  163.9 46.6 %backward_taps.1 = (bf16[432,512]{1,0:T(8,128)(2,1)}, bf16[28,512,256]{2,1,0:T(8,128)(2,1)}) custom-call(bf16[3,256,1152]{2,1,0:T(8,128)(2,1)} %bitcast.45, bf16[12,864,1024]{2,1,0:T(8,128)(2,1)} %get-tuple-element.25.b_ref, bf16[512,256]{1,0:T(8,128)(2,1)} %wp_ref.3, bf16[27,512,256]{2,1,0:T(8,128)(2,1)} %bitcast.42), custom_call_target="tpu_custom_call" | custom-call | tf_op jit(solution)/shard_map/backward_taps/pallas_call | solution.py:642
  210.4 1.0 slice_bitcast_fusion
  211.5 0.9 reshape.68
  212.4 1.7 slice_bitcast_fusion.1
  214.1 6.7 %slice.50 = bf16[27,512,256]{2,1,0:T(8,128)(2,1)} slice(bf16[28,512,256]{2,1,0:T(8,128)(2,1)} %get-tuple-element.27), slice={[1:28], [0:512], [0:256]} | slice | bytes 14155776 | tf_op jit(solution)/shard_map/slice | solution.py:731
  (6 shorter events, 0.1 us)
